TPU v7x, 32 devices: a whole 2x2x4 slice. The times are simulated.
32 devices in a mesh: rep: 8 (over y, x, core), tp: 4 (over z).
Axes of the slice: x: 2, y: 2, z: 4, core: 2. Of those that a mesh axis runs over, the one named last changes fastest.
Arguments:
- tokens: bfloat16 [4096, 8192], P('rep', 'tp'), may hold values from -6 to 6
- query_weight: bfloat16 [8192, 4096], P(None, 'tp'), may hold values from -0.0625 to 0.0625
- key_value_weight: bfloat16 [8192, 1024], P('tp'), may hold values from -0.0625 to 0.0625
- adapter_down_tables: bfloat16 [32, 192, 8192], P('rep', None, 'tp'), may hold values from -0.0625 to 0.0625
- adapter_up_query: bfloat16 [32, 64, 4096], P('rep', None, 'tp'), may hold values from -0.75 to 0.75
- adapter_up_key_value: bfloat16 [32, 64, 1024], P('rep', None, 'tp'), may hold values from -0.75 to 0.75
- request_adapter: int32 [128], P('rep'), may hold values from 0 to 31, as said below
- request_token_length: int32 [128], P('rep'), may hold values from 8 to 32, as said below
- adapter_table_row: int32 [32], replicated, may hold values from 0 to 31, as said below
Outputs:
- attended: bfloat16 [4096, 4096], P('rep', 'tp')
Inputs may be any that keep to these rules, and one draw needn't show every extreme that they name: `request_adapter`: in each replica's block of 16 requests at most 4 have adapters whose table rows adapter_table_row lies in one index of rep's share (rows s with the same s // 4); in every draw one share gets exactly 4 from every replica. `adapter_table_row`: A permutation of the table rows. `request_token_length`: every replica has one request of exactly 32 tokens.
All inputs are finite; a program needn't handle non-finite values.
Results may differ from a plain program's by a relative error of at most 0.0098.
Values may be sent and summed in bfloat16 or wider, within the bound.
A program may use at most 192 MiB of HBM per device.

v0:
```python
import math

import jax
import jax.numpy as jnp
from jax import lax
from jax.sharding import PartitionSpec as P

HEAD_SIZE = 128


adapter_scale = 0.5
rope_theta = 500000.0


def rotary(values, positions):
    half_dim = values.shape[-1] // 2
    frequency = rope_theta ** (-(jnp.arange(half_dim, dtype=jnp.float32) * 2.0 / values.shape[-1]))
    angles = positions.astype(jnp.float32)[:, None] * frequency[None, :]
    cosine = jnp.cos(angles)[:, None, :]
    sine_part = jnp.sin(angles)[:, None, :]
    lower_half = values[..., :half_dim]
    upper_half = values[..., half_dim:]
    return jnp.concatenate(
        [
            lower_half * cosine - upper_half * sine_part,
            upper_half * cosine + lower_half * sine_part,
        ],
        axis=-1,
    )


def expand_slots(shrink, query_up_weight, key_value_up_weight, value_side):
    rank_size = query_up_weight.shape[2]
    query_change = jnp.einsum(
        "sinr,sirc->sinc",
        shrink[..., :rank_size],
        query_up_weight,
        preferred_element_type=jnp.float32,
    )
    pair_input = jnp.where(
        value_side, shrink[..., 2 * rank_size :], shrink[..., rank_size : 2 * rank_size]
    )
    key_value_update = jnp.einsum(
        "sinr,sirc->sinc", pair_input, key_value_up_weight, preferred_element_type=jnp.float32
    )
    return (adapter_scale * jnp.concatenate([query_change, key_value_update], axis=-1)).astype(
        jnp.bfloat16
    )


def shards(
    tokens,
    query_weight,
    key_value_weight,
    adapter_down_tables,
    adapter_up_query,
    adapter_up_key_value,
    request_adapter,
    request_token_length,
    adapter_table_row,
):
    replicas = lax.axis_size("rep")
    tp_count = lax.axis_size("tp")
    tp_here = lax.axis_index("tp")
    tok_rows = tokens.shape[0]
    feat_local = tokens.shape[1]
    query_cols = query_weight.shape[1]
    pair_total = key_value_weight.shape[1]
    portion_value = adapter_up_key_value.shape[2]
    local_table_rows = adapter_down_tables.shape[0]
    requests_here = request_adapter.shape[0]
    seq_len = tok_rows // requests_here
    capacity = max(1, 2 * requests_here // replicas)
    slot_count = replicas * capacity
    delta_cols = query_cols + portion_value
    value_side = tp_here >= tp_count // 2
    base_query = jnp.dot(
        lax.all_gather(tokens, "tp", axis=1, tiled=True),
        query_weight,
        preferred_element_type=jnp.float32,
    )
    base_pair = jnp.dot(tokens, key_value_weight, preferred_element_type=jnp.float32)
    id_match = (
        request_adapter[:, None] == jnp.arange(adapter_table_row.shape[0], dtype=jnp.int32)[None, :]
    )
    homes = jnp.sum(jnp.where(id_match, adapter_table_row[None, :], 0), axis=1)
    owners = homes // local_table_rows
    local_ids = homes % local_table_rows
    request_pos = jnp.arange(requests_here, dtype=jnp.int32)
    earlier = (owners[:, None] == owners[None, :]) & (request_pos[None, :] < request_pos[:, None])
    slot_ids = owners * capacity + jnp.sum(earlier.astype(jnp.int32), axis=1)
    placement = slot_ids[None, :] == jnp.arange(slot_count, dtype=jnp.int32)[:, None]
    place_matrix = placement.astype(jnp.bfloat16)
    send_rows = jnp.dot(
        place_matrix,
        tokens.reshape(requests_here, seq_len * feat_local),
        preferred_element_type=jnp.float32,
    )
    send_rows = send_rows.astype(jnp.bfloat16).reshape(replicas, capacity, seq_len, feat_local)
    slot_local = jnp.sum(jnp.where(placement, local_ids[None, :], 0), axis=1).reshape(
        replicas, capacity
    )
    needed_locally = lax.all_to_all(slot_local, "rep", split_axis=0, concat_axis=0, tiled=True)
    fetched_down, fetched_query, fetched_pair = (
        lax.all_to_all(
            jnp.take(adapter_down_tables, needed_locally, axis=0),
            "rep",
            split_axis=0,
            concat_axis=0,
            tiled=True,
        ),
        lax.all_to_all(
            jnp.take(adapter_up_query, needed_locally, axis=0),
            "rep",
            split_axis=0,
            concat_axis=0,
            tiled=True,
        ),
        lax.all_to_all(
            jnp.take(adapter_up_key_value, needed_locally, axis=0),
            "rep",
            split_axis=0,
            concat_axis=0,
            tiled=True,
        ),
    )
    partial_sum = jnp.einsum(
        "scnf,scrf->scnr", send_rows, fetched_down, preferred_element_type=jnp.float32
    )
    shrink = lax.psum(partial_sum, "tp").astype(jnp.bfloat16)
    returned = expand_slots(shrink, fetched_query, fetched_pair, value_side)
    delta = jnp.dot(
        place_matrix.T,
        returned.reshape(slot_count, seq_len * delta_cols),
        preferred_element_type=jnp.float32,
    )
    delta = delta.reshape(tok_rows, delta_cols)
    positions = jnp.arange(tok_rows, dtype=jnp.int32) % seq_len
    heads_here = query_cols // HEAD_SIZE
    query = rotary(
        (base_query + delta[:, :query_cols]).reshape(tok_rows, heads_here, HEAD_SIZE), positions
    ).astype(jnp.bfloat16)
    placed = lax.dynamic_update_slice_in_dim(
        jnp.zeros((tok_rows, pair_total), jnp.float32),
        delta[:, query_cols:],
        tp_here * portion_value,
        1,
    )
    pair_full = lax.psum(base_pair + placed, "tp")
    pair_raw = lax.optimization_barrier(pair_full.astype(jnp.bfloat16))
    kv_heads = pair_total // (2 * HEAD_SIZE)
    head_index = tp_here // (tp_count // kv_heads)
    keys_raw = lax.dynamic_slice_in_dim(pair_raw, head_index * HEAD_SIZE, HEAD_SIZE, 1)
    values = lax.dynamic_slice_in_dim(
        pair_raw, kv_heads * HEAD_SIZE + head_index * HEAD_SIZE, HEAD_SIZE, 1
    )
    keys = rotary(keys_raw.astype(jnp.float32).reshape(tok_rows, 1, HEAD_SIZE), positions).astype(
        jnp.bfloat16
    )
    query_blocks = query.reshape(requests_here, seq_len, heads_here, HEAD_SIZE)
    key_blocks = keys.reshape(requests_here, seq_len, HEAD_SIZE)
    value_blocks = values.reshape(requests_here, seq_len, HEAD_SIZE)
    scores = jnp.einsum(
        "rqhd,rpd->rhqp", query_blocks, key_blocks, preferred_element_type=jnp.float32
    ) / math.sqrt(HEAD_SIZE)
    slot_pos = jnp.arange(seq_len, dtype=jnp.int32)
    allowed = (slot_pos[None, None, :] <= slot_pos[None, :, None]) & (
        slot_pos[None, None, :] < request_token_length[:, None, None]
    )
    scores = jnp.where(allowed[:, None, :, :], scores, jnp.float32(-1e30))
    peak = jnp.max(scores, axis=-1, keepdims=True)
    weights = jnp.exp(scores - peak)
    probs = (weights / jnp.sum(weights, axis=-1, keepdims=True)).astype(jnp.bfloat16)
    mixed = jnp.einsum("rhqp,rpd->rqhd", probs, value_blocks, preferred_element_type=jnp.float32)
    live = slot_pos[None, :] < request_token_length[:, None]
    mixed = jnp.where(live[:, :, None, None], mixed, jnp.float32(0.0))
    return mixed.astype(jnp.bfloat16).reshape(tok_rows, query_cols)


def solution(mesh):
    placed = (
        P("rep", "tp"),
        P(None, "tp"),
        P("tp", None),
        P("rep", None, "tp"),
        P("rep", None, "tp"),
        P("rep", None, "tp"),
        P("rep"),
        P("rep"),
        P(),
    )
    return jax.shard_map(
        shards, mesh=mesh, in_specs=placed, out_specs=P("rep", "tp"), check_vma=False
    )
```

profile of v0, /device:TPU:0, one launch (start us, length us, event | category | flops | bytes accessed | tf_op | source)
XLA Modules:
  0.0 532.3 jit_solution(14135804955367768476)
XLA Ops:
  7.9 9.6 %all_to_all.30 = s32[8,1,4]{2,1,0:T(1,128)S(1)} all-to-all(s32[8,1,4]{2,1,0:T(1,128)S(1)} %bitcast.83), channel_id=1, replica_groups=mesh['rep'=8,'tp'=4] {'rep'}, dimensions={0} | all-to-all | bytes 256 | tf_op jit(solution)/shard_map/all_to_all | solution.py:103
  17.9 10.0 %gather_fusion = bf16[32,192,2048]{2,1,0:T(8,128)(2,1)} fusion(bf16[4,192,2048]{2,1,0:T(8,128)(2,1)S(1)} %copy-done, s32[1024]{0:T(1024)S(1)} %pad_clamp_fusion), kind=kCustom, calls=%fused_computation | custom fusion | bytes 50331776 | tf_op jit(solution)/shard_map/jit(_take)/gather | solution.py:106
  29.6 3.6 all-to-all-start.3
  33.2 21.2 %broadcast_select_fusion = bf16[8,4,192,2048]{3,2,1,0:T(8,128)(2,1)} fusion(bf16[8,4,192,2048]{3,2,1,0:T(8,128)(2,1)} %bitcast.69, pred[8,4]{1,0:T(8,128)(4,1)S(1)} %copy.40), kind=kLoop, calls=%fused_computation.5 | loop fusion | flops 12582912 | bytes 50331680 | tf_op jit(solution)/shard_map/jit(_take)/select_n | solution.py:106
  55.4 6.4 %all-to-all-start.1 = ((bf16[8,4,192,2048]{3,2,1,0:T(8,128)(2,1)}), bf16[8,4,192,2048]{3,2,1,0:T(8,128)(2,1)}, u32[]{:S(2)}, u32[]{:S(2)}) async-start(bf16[8,4,192,2048]{3,2,1,0:T(8,128)(2,1)} %broadcast_select_fusion), calls=%async_computation.1 | async-start | bytes 50331648 | tf_op jit(solution)/shard_map/all_to_all | solution.py:105
  62.6 2.2 reshape.310
  64.9 3.3 convolution_convert_fusion
  68.2 2.8 gather_fusion.1
  71.0 5.1 broadcast_select_fusion.1
  76.0 259.6 %all-to-all-done.1 = bf16[8,4,192,2048]{3,2,1,0:T(8,128)(2,1)} async-done(((bf16[8,4,192,2048]{3,2,1,0:T(8,128)(2,1)}), bf16[8,4,192,2048]{3,2,1,0:T(8,128)(2,1)}, u32[]{:S(2)}, u32[]{:S(2)}) %all-to-all-start.1) | async-done | bytes 25165856 | tf_op jit(solution)/shard_map/all_to_all | solution.py:105
  335.6 4.8 all-to-all-start.2
  340.5 6.6 %copy.52 = bf16[4,8,32,2048]{3,2,1,0:T(8,128)(2,1)} copy(bf16[4,8,32,2048]{3,1,2,0:T(8,128)(2,1)} %bitcast.71) | data formatting | bytes 8388608
  349.6 5.8 %fusion.48 = f32[512,1024]{1,0:T(8,128)} fusion(bf16[512,2048]{1,0:T(8,128)(2,1)S(1)} %copy-done.3, bf16[2048,1024]{1,0:T(8,128)(2,1)} %param.11), kind=kOutput, calls=%fused_computation.86 | convolution fusion | flops 2147483648 | bytes 8388608 | tf_op jit(solution)/shard_map/dot_general | solution.py:82
  355.4 13.4 %fusion.49 = f32[8,4,32,192]{3,2,1,0:T(8,128)S(1)} fusion(bf16[8,4,32,2048]{3,2,1,0:T(8,128)(2,1)} %bitcast.73, bf16[8,4,192,2048]{3,2,1,0:T(8,128)(2,1)} %all-to-all-done.1), kind=kOutput, calls=%fused_computation.87 | convolution fusion | flops 805306368 | bytes 30146560 | tf_op jit(solution)/shard_map/scnf,scrf->scnr/dot_general | solution.py:127
  368.9 43.8 %all-reduce.2 = bf16[8,4,32,192]{3,2,1,0:T(8,128)(2,1)S(1)} all-reduce(f32[8,4,32,192]{3,2,1,0:T(8,128)S(1)} %fusion.49), channel_id=1, replica_groups=mesh['rep'=8,'tp'=4] {'tp'}, use_global_device_ids=true, to_apply=%region_3.4 | all-reduce | flops 196608 | bytes 1179648 | tf_op jit(solution)/shard_map/psum | solution.py:130
  413.1 2.9 fusion.23
  418.1 2.1 fusion.32
  420.2 1.9 reshape.312
  422.1 2.0 fusion.12
  424.1 72.7 %all-reduce.3 = bf16[512,1024]{1,0:T(8,128)(2,1)} all-reduce(f32[512,1024]{1,0:T(8,128)} %fusion.12), channel_id=1, replica_groups=mesh['rep'=8,'tp'=4] {'tp'}, use_global_device_ids=true, to_apply=%region_4.5 | all-reduce | flops 524288 | bytes 3145728 | tf_op jit(solution)/shard_map/psum | solution.py:149
  497.8 1.9 fusion.18
  499.6 14.4 %fusion.2 = f32[64,8,8,128]{3,1,2,0:T(8,128)S(1)} fusion(f32[512,1280]{1,0:T(8,128)S(1)} %reshape.312, bf16[512,8192]{1,0:T(8,128)(2,1)} %all-gather.2.cloned.1.call-done, bf16[8192,1024]{1,0:T(8,128)(2,1)} %param.10), kind=kOutput, calls=%fused_computation.10 | convolution fusion | flops 8590458880 | bytes 29360128 | tf_op jit(solution)/shard_map/dot_general | solution.py:77
  516.7 4.7 fusion.45
  521.5 2.3 fusion.4
  (58 shorter events, 15.7 us)
Async XLA Ops:
  6.5 11.4 %copy-start = (bf16[4,192,2048]{2,1,0:T(8,128)(2,1)S(1)}, bf16[4,192,2048]{2,1,0:T(8,128)(2,1)}, u32[]{:S(2)}) copy-start(bf16[4,192,2048]{2,1,0:T(8,128)(2,1)} %param.12) | copy-start | bytes 9437188
  17.9 10.0 %copy-start.4 = (bf16[4,64,256]{2,1,0:T(8,128)(2,1)S(1)}, bf16[4,64,256]{2,1,0:T(8,128)(2,1)}, u32[]{:S(2)}) copy-start(bf16[4,64,256]{2,1,0:T(8,128)(2,1)} %param.14) | copy-start | bytes 393220
  29.6 24.8 %all-to-all-start.3 = ((bf16[8,4,64,256]{3,2,1,0:T(8,128)(2,1)}), bf16[8,4,64,256]{3,2,1,0:T(8,128)(2,1)S(1)}, u32[]{:S(2)}, u32[]{:S(2)}) async-start(bf16[8,4,64,256]{3,2,1,0:T(8,128)(2,1)} %broadcast_select_fusion.2), calls=%async_computation.3 | async-start | bytes 2097152 | tf_op jit(solution)/shard_map/all_to_all | solution.py:119
  54.4 1.0 copy-start.5
  55.4 280.3 %all-to-all-start.1 = ((bf16[8,4,192,2048]{3,2,1,0:T(8,128)(2,1)}), bf16[8,4,192,2048]{3,2,1,0:T(8,128)(2,1)}, u32[]{:S(2)}, u32[]{:S(2)}) async-start(bf16[8,4,192,2048]{3,2,1,0:T(8,128)(2,1)} %broadcast_select_fusion), calls=%async_computation.1 | async-start | bytes 50331648 | tf_op jit(solution)/shard_map/all_to_all | solution.py:105
  61.8 437.8 %all-gather.2.cloned.1.call-start = ((), (), s32[]{:S(2)}) async-start(), calls=%async_computation.4 | async-start | bytes 10485760 | tf_op jit(solution)/shard_map/all_gather | solution.py:78
  62.5 2.3 copy-start.10
  64.9 3.3 copy-start.2
  335.6 77.4 %all-to-all-start.2 = ((bf16[8,4,64,1024]{3,2,1,0:T(8,128)(2,1)}), bf16[8,4,64,1024]{3,2,1,0:T(8,128)(2,1)}, u32[]{:S(2)}, u32[]{:S(2)}) async-start(bf16[8,4,64,1024]{3,2,1,0:T(8,128)(2,1)} %broadcast_select_fusion.1), calls=%async_computation.2 | async-start | bytes 8388608 | tf_op jit(solution)/shard_map/all_to_all | solution.py:112
  340.4 9.1 %copy-start.3 = (bf16[512,2048]{1,0:T(8,128)(2,1)S(1)}, bf16[512,2048]{1,0:T(8,128)(2,1)}, u32[]{:S(2)}) copy-start(bf16[512,2048]{1,0:T(8,128)(2,1)} %param.9) | copy-start | bytes 6291460
  355.4 57.3 %copy-start.6 = (bf16[8,4,64,256]{3,2,1,0:T(8,128)(2,1)S(1)}, bf16[8,4,64,256]{3,2,1,0:T(8,128)(2,1)}, u32[]{:S(2)}) copy-start(bf16[8,4,64,256]{3,2,1,0:T(8,128)(2,1)} %copy-done.5) | copy-start | bytes 3145732
  514.0 1.0 copy-start.7
  515.8 0.9 copy-start.8
  515.8 1.0 copy-start.9
  521.4 4.0 copy-start.1
Sparse Core Ops, SparseCore 0:
  64.2 151.2 all-gather.1
where the time goes:
time: 533 us; the launch traced here: 532 us
  waiting for transfers between devices  260 us (49%)
  blocking collectives  126 us (24%)
  matrix products  49.3 us (9%)
  other arithmetic  37.6 us (7%)
  local copies, waits for them, and re-layouts  30.6 us (6%)
  starting transfers between devices  14.8 us (3%)
  between operations  13.6 us (3%)
    all_to_all x1, waiting for transfers between devices, shards(): lax.all_to_all(jnp.take(adapter_down_tables, needed_locally, axis=0), 're...  260 us
    psum x1, blocking collectives, shards(): pair_full = lax.psum(base_pair + placed, 'tp')  72.7 us
    psum x1, blocking collectives, shards(): shrink = lax.psum(partial_sum, 'tp').astype(jnp.bfloat16)  43.8 us
    select_n x2, other arithmetic, shards(): jnp.take(adapter_down_tables, needed_locally, axis=0)  21.2 us
    dot_general x1, matrix products, shards(): jnp.dot(lax.all_gather(tokens, 'tp', axis=1, tiled=True), query_weight, p...  14.4 us
    dot_general x1, matrix products, shards(): jnp.einsum('scnf,scrf->scnr', send_rows, fetched_down, preferred_element_...  13.4 us
    unnamed x26, local copies, waits for them, and re-layouts  11.7 us
  transfers between devices with their start and end apart: 4, of which 1 were waited for; matrix products, arithmetic and copies ran while one was open for 15% of the time, Pallas kernels for 0%

commit v1 on v0

v1 whole, which is shorter than its diff:
```python
import math

import jax
import jax.numpy as jnp
import numpy as np
from jax import lax
from jax.experimental import pallas as pl
from jax.experimental.pallas import tpu as pltpu
from jax.sharding import PartitionSpec as P

HEAD_SIZE = 128
HALF = HEAD_SIZE // 2

adapter_scale = 0.5
rope_theta = 500000.0


def rope_tables(seq_len, rows):
    frequency = np.float64(rope_theta) ** (-(np.arange(HALF, dtype=np.float64) * 2.0 / HEAD_SIZE))
    angles = (np.arange(rows) % seq_len).astype(np.float64)[:, None] * frequency[None, :]
    cosine = np.concatenate([np.cos(angles), np.cos(angles)], axis=1)
    sine = np.concatenate([-np.sin(angles), np.sin(angles)], axis=1)
    return cosine.astype(np.float32), sine.astype(np.float32)


def attend_kernel(seq_len, per_block, heads_here, slots, lengths, base, pair, delta, cosine, sine, out):
    block = pl.program_id(0)
    rows = per_block * seq_len
    query_cols = heads_here * HEAD_SIZE
    picked = [slots[block * per_block + j] for j in range(per_block)]
    sizes = [lengths[block * per_block + j] for j in range(per_block)]

    def change(start, width):
        return jnp.concatenate(
            [delta[s, :, start : start + width] for s in picked], axis=0
        ).astype(jnp.float32)

    cos = cosine[...]
    sin = sine[...]

    def rotate(v):
        return (v * cos + pltpu.roll(v, HALF, 1) * sin).astype(jnp.bfloat16)

    keys_raw = (pair[:, :HEAD_SIZE] + change(query_cols, HEAD_SIZE)).astype(jnp.bfloat16)
    values = (pair[:, HEAD_SIZE:] + change(query_cols + HEAD_SIZE, HEAD_SIZE)).astype(jnp.bfloat16)
    keys = rotate(keys_raw.astype(jnp.float32))
    q_at = lax.broadcasted_iota(jnp.int32, (rows, rows), 0)
    p_at = lax.broadcasted_iota(jnp.int32, (rows, rows), 1)
    p_request = p_at // seq_len
    q_row = lax.broadcasted_iota(jnp.int32, (rows, HEAD_SIZE), 0)
    limit = jnp.zeros((rows, rows), jnp.int32)
    q_limit = jnp.zeros((rows, HEAD_SIZE), jnp.int32)
    for j in range(per_block):
        limit = jnp.where(p_request == j, sizes[j] + j * seq_len, limit)
        q_limit = jnp.where(q_row // seq_len == j, sizes[j] + j * seq_len, q_limit)
    allowed = (p_request == q_at // seq_len) & (p_at <= q_at) & (p_at < limit)
    live = q_row < q_limit
    for h in range(heads_here):
        at = h * HEAD_SIZE
        query = rotate(base[:, at : at + HEAD_SIZE] + change(at, HEAD_SIZE))
        scores = lax.dot_general(
            query, keys, (((1,), (1,)), ((), ())), preferred_element_type=jnp.float32
        ) * (1.0 / math.sqrt(HEAD_SIZE))
        scores = jnp.where(allowed, scores, jnp.float32(-1e30))
        weights = jnp.exp(scores - jnp.max(scores, axis=1, keepdims=True))
        probs = (weights / jnp.sum(weights, axis=1, keepdims=True)).astype(jnp.bfloat16)
        mixed = jnp.dot(probs, values, preferred_element_type=jnp.float32)
        out[:, at : at + HEAD_SIZE] = jnp.where(live, mixed, 0.0).astype(jnp.bfloat16)


def attend(slots, lengths, base, pair, delta, seq_len):
    tok_rows, query_cols = base.shape
    per_block = max(1, HEAD_SIZE // seq_len)
    rows = per_block * seq_len
    cosine, sine = rope_tables(seq_len, rows)
    whole = lambda shape: pl.BlockSpec(shape, lambda i, *_: (0,) * len(shape))
    part = lambda cols: pl.BlockSpec((rows, cols), lambda i, *_: (i, 0))

    def body(*refs):
        attend_kernel(seq_len, per_block, query_cols // HEAD_SIZE, *refs)

    return pl.pallas_call(
        body,
        out_shape=jax.ShapeDtypeStruct((tok_rows, query_cols), jnp.bfloat16),
        grid_spec=pltpu.PrefetchScalarGridSpec(
            num_scalar_prefetch=2,
            grid=(tok_rows // rows,),
            in_specs=[
                part(query_cols),
                part(2 * HEAD_SIZE),
                whole(delta.shape),
                whole(cosine.shape),
                whole(sine.shape),
            ],
            out_specs=part(query_cols),
        ),
        compiler_params=pltpu.CompilerParams(vmem_limit_bytes=32 << 20),
    )(slots, lengths, base, pair, delta, jnp.asarray(cosine), jnp.asarray(sine))


def shards(
    tokens,
    query_weight,
    key_value_weight,
    adapter_down_tables,
    adapter_up_query,
    adapter_up_key_value,
    request_adapter,
    request_token_length,
    adapter_table_row,
):
    replicas = lax.axis_size("rep")
    tp_count = lax.axis_size("tp")
    tp_here = lax.axis_index("tp")
    rep_here = lax.axis_index("rep")
    tok_rows, feat_local = tokens.shape
    query_cols = query_weight.shape[1]
    pair_total = key_value_weight.shape[1]
    local_rows = adapter_down_tables.shape[0]
    rank = adapter_up_query.shape[1]
    requests_here = request_adapter.shape[0]
    seq_len = tok_rows // requests_here
    capacity = max(1, 2 * requests_here // replicas)
    slot_count = replicas * capacity
    kv_heads = pair_total // (2 * HEAD_SIZE)
    sharing = tp_count // kv_heads

    everyone = lax.all_gather(request_adapter, "rep", axis=0, tiled=False)
    match = everyone[:, :, None] == jnp.arange(adapter_table_row.shape[0], dtype=jnp.int32)
    homes = jnp.sum(jnp.where(match, adapter_table_row, 0), axis=2)
    own_match = request_adapter[:, None] == jnp.arange(adapter_table_row.shape[0], dtype=jnp.int32)
    own_homes = jnp.sum(jnp.where(own_match, adapter_table_row, 0), axis=1)
    pos = jnp.arange(requests_here, dtype=jnp.int32)
    before = pos[None, :] < pos[:, None]
    own_owner = own_homes // local_rows
    own_earlier = (own_owner[:, None] == own_owner[None, :]) & before
    slot_ids = own_owner * capacity + jnp.sum(own_earlier.astype(jnp.int32), axis=1)
    slot_at = jnp.arange(slot_count, dtype=jnp.int32)
    slot_request = jnp.sum(jnp.where(slot_ids[None, :] == slot_at[:, None], pos, 0), axis=1)

    send = jnp.take(tokens.reshape(requests_here, seq_len, feat_local), slot_request, axis=0)
    received = lax.all_to_all(send, "rep", split_axis=0, concat_axis=0, tiled=True)
    received = received.reshape(slot_count * seq_len, feat_local)

    owners = homes // local_rows
    earlier = (owners[:, :, None] == owners[:, None, :]) & before[None]
    rank_in = jnp.sum(earlier.astype(jnp.int32), axis=2)
    cap_at = jnp.arange(capacity, dtype=jnp.int32)
    mine = (owners == rep_here)[:, None, :] & (rank_in[:, None, :] == cap_at[None, :, None])
    local = jnp.sum(jnp.where(mine, (homes % local_rows)[:, None, :], 0), axis=2)
    local_row = jnp.broadcast_to(
        local.reshape(slot_count, 1), (slot_count, seq_len)
    ).reshape(slot_count * seq_len, 1)

    base_pair = jnp.dot(tokens, key_value_weight, preferred_element_type=jnp.float32)
    side = kv_heads * HEAD_SIZE
    pieces = []
    for t in range(tp_count):
        at = (t // sharing) * HEAD_SIZE
        pieces.append(
            jnp.concatenate(
                [base_pair[:, at : at + HEAD_SIZE], base_pair[:, side + at : side + at + HEAD_SIZE]],
                axis=1,
            )
        )
    pair_here = lax.psum_scatter(jnp.stack(pieces), "tp", scatter_dimension=0, tiled=False)

    up_all = lax.all_gather(adapter_up_key_value, "tp", axis=2, tiled=True)
    head = tp_here // sharing
    up_key = lax.dynamic_slice_in_dim(up_all, head * HEAD_SIZE, HEAD_SIZE, 2)
    up_value = lax.dynamic_slice_in_dim(up_all, side + head * HEAD_SIZE, HEAD_SIZE, 2)

    gathered = lax.all_gather(tokens, "tp", axis=0, tiled=False)
    base_query = jnp.einsum(
        "tnf,tfc->nc",
        gathered,
        query_weight.reshape(tp_count, feat_local, query_cols),
        preferred_element_type=jnp.float32,
    )

    partial = jnp.zeros((slot_count * seq_len, 3 * rank), jnp.float32)
    for a in range(local_rows):
        one = lax.dot_general(
            received,
            adapter_down_tables[a],
            (((1,), (1,)), ((), ())),
            preferred_element_type=jnp.float32,
        )
        partial = jnp.where(local_row == a, one, partial)
    partials = lax.all_gather(partial.astype(jnp.bfloat16), "tp", axis=0, tiled=False)
    shrink = jnp.sum(partials.astype(jnp.float32), axis=0).astype(jnp.bfloat16)

    def expand(part, up):
        spread = jnp.concatenate(
            [jnp.where(local_row == a, part, jnp.bfloat16(0)) for a in range(local_rows)], axis=1
        )
        return jnp.dot(
            spread, up.reshape(local_rows * rank, up.shape[2]), preferred_element_type=jnp.float32
        )

    delta = jnp.concatenate(
        [
            expand(shrink[:, :rank], adapter_up_query),
            expand(shrink[:, rank : 2 * rank], up_key),
            expand(shrink[:, 2 * rank :], up_value),
        ],
        axis=1,
    )
    delta = (adapter_scale * delta).astype(jnp.bfloat16)
    returned = lax.all_to_all(
        delta.reshape(slot_count, seq_len, delta.shape[1]),
        "rep",
        split_axis=0,
        concat_axis=0,
        tiled=True,
    )
    return attend(slot_ids, request_token_length, base_query, pair_here, returned, seq_len)


def solution(mesh):
    placed = (
        P("rep", "tp"),
        P(None, "tp"),
        P("tp", None),
        P("rep", None, "tp"),
        P("rep", None, "tp"),
        P("rep", None, "tp"),
        P("rep"),
        P("rep"),
        P(),
    )
    return jax.shard_map(
        shards, mesh=mesh, in_specs=placed, out_specs=P("rep", "tp"), check_vma=False
    )
```

time: 533 us -> 354 us (0.66)
  waiting for transfers between devices: 260 us -> 180 us
  blocking collectives: 126 us -> 73.6 us
  other arithmetic: 37.6 us -> 13 us
  local copies, waits for them, and re-layouts: 30.6 us -> 13.1 us
  Pallas kernels: 0 us -> 12.7 us
  matrix products: 49.3 us -> 37.8 us
  starting transfers between devices: 14.8 us -> 9.07 us
    all_to_all x3 -> x2, waiting for transfers between devices: 260 us -> 0.01 us  [the longest x1 0.01 us: shards(): lax.all_to_all(send, 'rep', split_axis=0, concat_axis=0, tiled=True)]
    all_gather x1 -> x2, waiting for transfers between devices: 0.01 us -> 151 us  [the longest x1 136 us: shards(): gathered = lax.all_gather(tokens, 'tp', axis=0, tiled=False)]
    psum x2 -> x0, blocking collectives: 117 us -> none  [the longest x1 72.7 us: shards(): pair_full = lax.psum(base_pair + placed, 'tp')]
    unnamed x0 -> x1, blocking collectives: none -> 49.8 us
    reduce_scatter x0 -> x1, waiting for transfers between devices: none -> 28.5 us  [shards(): lax.psum_scatter(jnp.stack(pieces), 'tp', scatter_dimension=0, tiled=False)]
    all_gather x0 -> x1, blocking collectives: none -> 23.8 us  [shards(): up_all = lax.all_gather(adapter_up_key_value, 'tp', axis=2, tiled=True)]
    select_n x5, other arithmetic: 27.4 us -> 4.8 us  [the longest x2 4.63 us: shards(): jnp.take(tokens.reshape(requests_here, seq_len, feat_local), slot_request...]
    pallas_call x0 -> x1, Pallas kernels: none -> 12.7 us  [attend(): pl.pallas_call(body, out_shape=jax.ShapeDtypeStruct((tok_rows, query_cols...]
  transfers between devices with their start and end apart: 4 -> 5, of which waited for: 1 -> 3; matrix products, arithmetic and copies ran while one was open for 15% -> 10% of each run, Pallas kernels for 0% -> 0%
where the time goes in v1:
time: 354 us; the launch traced here: 353 us
  waiting for transfers between devices  180 us (51%)
  blocking collectives  73.6 us (21%)
  matrix products  37.8 us (11%)
  between operations  14.1 us (4%)
  local copies, waits for them, and re-layouts  13.1 us (4%)
  other arithmetic  13 us (4%)
  Pallas kernels  12.7 us (4%)
  starting transfers between devices  9.07 us (3%)
    all_gather x1, waiting for transfers between devices, shards(): gathered = lax.all_gather(tokens, 'tp', axis=0, tiled=False)  136 us
    unnamed x1, blocking collectives  49.8 us
    reduce_scatter x1, waiting for transfers between devices, shards(): lax.psum_scatter(jnp.stack(pieces), 'tp', scatter_dimension=0, tiled=False)  28.5 us
    all_gather x1, blocking collectives, shards(): up_all = lax.all_gather(adapter_up_key_value, 'tp', axis=2, tiled=True)  23.8 us
    dot_general x4, matrix products, shards(): lax.dot_general(received, adapter_down_tables[a], (((1,), (1,)), ((), ())...  16.1 us
    dot_general x1, matrix products, shards(): jnp.einsum('tnf,tfc->nc', gathered, query_weight.reshape(tp_count, feat_l...  15.9 us
    all_gather x1, waiting for transfers between devices, shards(): lax.all_gather(partial.astype(jnp.bfloat16), 'tp', axis=0, tiled=False)  14.9 us
    pallas_call x1, Pallas kernels, attend(): pl.pallas_call(body, out_shape=jax.ShapeDtypeStruct((tok_rows, query_cols...  12.7 us
  transfers between devices with their start and end apart: 5, of which 3 were waited for; matrix products, arithmetic and copies ran while one was open for 10% of the time, Pallas kernels for 0%

profile of v1, /device:TPU:0, one launch (start us, length us, event | category | flops | bytes accessed | tf_op | source)
XLA Modules:
  0.0 353.4 jit_solution(6111970999760748726)
XLA Ops:
  6.5 0.9 select_reduce_fusion.3
  7.8 4.4 %gather_fusion = bf16[32,32,2048]{2,1,0:T(8,128)(2,1)} fusion(bf16[16,32,2048]{2,1,0:T(8,128)(2,1)} %bitcast.62, s32[1024]{0:T(1024)S(1)} %pad_clamp_fusion), kind=kCustom, calls=%fused_computation | custom fusion | bytes 8388736 | tf_op jit(solution)/shard_map/jit(_take)/gather | solution.py:141
  12.2 4.6 %broadcast_select_fusion = bf16[32,32,2048]{2,1,0:T(8,128)(2,1)} fusion(bf16[32,32,2048]{2,1,0:T(8,128)(2,1)} %gather_fusion, pred[32]{0:T(512)(128)(4,1)S(1)} %compare_and_fusion), kind=kLoop, calls=%fused_computation.3 | loop fusion | flops 2097152 | bytes 8388640 | tf_op jit(solution)/shard_map/jit(_take)/select_n | solution.py:141
  16.8 5.3 %all-to-all-start = ((bf16[32,32,2048]{2,1,0:T(8,128)(2,1)}), bf16[32,32,2048]{2,1,0:T(8,128)(2,1)}, u32[]{:S(2)}, u32[]{:S(2)}) async-start(bf16[32,32,2048]{2,1,0:T(8,128)(2,1)} %broadcast_select_fusion), calls=%async_computation.1 | async-start | bytes 8388608 | tf_op jit(solution)/shard_map/all_to_all | solution.py:142
  23.7 49.8 %all-reduce = s32[128]{0:T(128)S(1)} all-reduce(s32[128]{0:T(128)S(1)} %dynamic-update-slice), channel_id=3, replica_groups=mesh['rep'=8,'tp'=4] {'rep'}, use_global_device_ids=true, to_apply=%add | all-reduce | flops 128 | bytes 1024
  75.8 4.1 %convolution_select_fusion = bf16[1024,192]{0,1:T(8,128)(2,1)S(1)} fusion(bf16[1024,2048]{1,0:T(8,128)(2,1)} %bitcast.12, bf16[4,192,2048]{2,1,0:T(8,128)(2,1)} %param.14, pred[1024]{0:T(1024)(128)(4,1)S(1)} %eq.181), kind=kOutput, calls=%fused_computation.6 | convolution fusion | flops 805502976 | bytes 5374976 | tf_op jit(solution)/shard_map/dot_general | solution.py:183
  79.9 3.7 %convolution_select_fusion.1 = bf16[1024,192]{0,1:T(8,128)(2,1)S(1)} fusion(bf16[1024,192]{0,1:T(8,128)(2,1)S(1)} %convolution_select_fusion, bf16[1024,2048]{1,0:T(8,128)(2,1)} %bitcast.12, bf16[4,192,2048]{2,1,0:T(8,128)(2,1)S(1)} %copy-done.9, pred[1024]{0:T(1024)(128)(4,1)S(1)} %eq.193), kind=kOutput, calls=%fused_computation.7 | convolution fusion | flops 805502976 | bytes 5768192 | tf_op jit(solution)/shard_map/dot_general | solution.py:183
  83.6 3.7 %convolution_select_fusion.2 = bf16[1024,192]{0,1:T(8,128)(2,1)S(1)} fusion(bf16[1024,192]{0,1:T(8,128)(2,1)S(1)} %convolution_select_fusion.1, bf16[1024,2048]{1,0:T(8,128)(2,1)} %bitcast.12, bf16[4,192,2048]{2,1,0:T(8,128)(2,1)S(1)} %copy-done.9, pred[1024]{0:T(1024)(128)(4,1)S(1)} %eq.190), kind=kOutput, calls=%fused_computation.8 | convolution fusion | flops 805502976 | bytes 5768192 | tf_op jit(solution)/shard_map/dot_general | solution.py:183
  87.3 4.6 %fusion.1 = bf16[1024,192]{0,1:T(8,128)(2,1)} fusion(bf16[1024,192]{0,1:T(8,128)(2,1)S(1)} %convolution_select_fusion.2, bf16[1024,2048]{1,0:T(8,128)(2,1)} %bitcast.12, bf16[4,192,2048]{2,1,0:T(8,128)(2,1)S(1)} %copy-done.9, pred[1024]{0:T(1024)(128)(4,1)S(1)} %eq.184), kind=kOutput, calls=%fused_computation.10 | convolution fusion | flops 805502976 | bytes 5768192 | tf_op jit(solution)/shard_map/dot_general | solution.py:183
  92.8 4.6 %fusion.15 = f32[512,1024]{1,0:T(8,128)S(1)} fusion(bf16[512,2048]{1,0:T(8,128)(2,1)S(1)} %copy-done.6, bf16[2048,1024]{1,0:T(8,128)(2,1)} %param.13), kind=kOutput, calls=%fused_computation.76 | convolution fusion | flops 2147483648 | bytes 8388608 | tf_op jit(solution)/shard_map/dot_general | solution.py:155
  97.7 1.5 pad_maximum_fusion
  99.3 23.8 %all_gather.27 = bf16[4,64,1024]{2,1,0:T(8,128)(2,1)S(1)} all-gather(bf16[4,64,256]{2,1,0:T(8,128)(2,1)S(1)} %copy-done.7), channel_id=1, replica_groups=mesh['rep'=8,'tp'=4] {'tp'}, dimensions={2}, use_global_device_ids=true | all-gather | bytes 655360 | tf_op jit(solution)/shard_map/all_gather | solution.py:168
  123.1 14.9 %all-gather.8.cloned.1.call-done = bf16[4096,192]{0,1:T(8,128)(2,1)} async-done(((bf16[1024,192]{0,1:T(8,128)(2,1)}), bf16[4096,192]{0,1:T(8,128)(2,1)}) %all-gather.8.cloned.1.call-update) | async-done | bytes 1572880 | tf_op jit(solution)/shard_map/all_gather | solution.py:190
  138.0 2.9 reshape.211
  140.9 2.2 reduce_sum.75
  144.6 0.7 fusion.16
  145.3 2.2 fusion
  147.5 3.7 %all-to-all-start.1 = ((bf16[32,32,1280]{2,1,0:T(8,128)(2,1)}), bf16[32,32,1280]{2,1,0:T(8,128)(2,1)S(1)}, u32[]{:S(2)}, u32[]{:S(2)}) async-start(bf16[32,32,1280]{2,1,0:T(8,128)(2,1)} %fusion), calls=%async_computation.2 | async-start | bytes 5242880 | tf_op jit(solution)/shard_map/all_to_all | solution.py:210
  151.2 136.0 %all-gather.6.cloned.1.call-done = bf16[2048,2048]{1,0:T(8,128)(2,1)} async-done(((bf16[512,2048]{1,0:T(8,128)(2,1)}), bf16[2048,2048]{1,0:T(8,128)(2,1)}) %all-gather.6.cloned.1.call-update) | async-done | bytes 8388624 | tf_op jit(solution)/shard_map/all_gather | solution.py:173
  287.2 15.9 %convolution_bitcast_fusion.refs_2_ = f32[512,1024]{1,0:T(8,128)} fusion(bf16[4,512,2048]{2,1,0:T(8,128)(2,1)} %bitcast.69, bf16[4,2048,1024]{2,1,0:T(8,128)(2,1)} %bitcast.68), kind=kOutput, calls=%fused_computation.5 | convolution fusion | flops 8589934592 | bytes 27262976 | tf_op jit(solution)/shard_map/tnf,tfc->nc/dot_general | solution.py:174
  303.1 28.5 %reduce-scatter.2.cloned.1.call-done = f32[1,512,256]{2,1,0:T(8,128)} async-done(((f32[4,512,256]{2,1,0:T(8,128)}), f32[1,512,256]{2,1,0:T(8,128)}) %reduce-scatter.2.cloned.1.call-update) | async-done | bytes 524304 | tf_op jit(solution)/shard_map/reduce_scatter | solution.py:166
  331.6 1.6 copy-done.1
  333.2 1.0 copy-done.2
  334.2 12.7 %shard_map.109 = bf16[512,1024]{1,0:T(8,128)(2,1)} custom-call(s32[16]{0:T(128)S(1)} %multiply_add_fusion.refs_0_, s32[16]{0:T(128)S(1)} %copy-done.5, f32[512,1024]{1,0:T(8,128)S(1)} %copy-done.1, f32[512,256]{1,0:T(8,128)S(1)} %bitcast.61, bf16[32,32,1280]{2,1,0:T(8,128)(2,1)S(1)} %all-to-all-done.1.refs_4_, f32[128,128]{1,0:T(8,128)S(1)} %copy-done.3, ...), custom_call_target="tpu_custom_call" | custom-call | tf_op jit(solution)/shard_map/pallas_call | solution.py:82
  (76 shorter events, 6.1 us)
Async XLA Ops:
  6.5 138.0 %copy-start = (bf16[4,64,1024]{2,1,0:T(8,128)(2,1)S(1)}, bf16[4,64,1024]{2,1,0:T(8,128)(2,1)}, u32[]{:S(2)}) copy-start(bf16[4,64,1024]{2,1,0:T(8,128)(2,1)} %param.15) | copy-start | bytes 1572868
  16.8 5.4 %copy-start.11 = (u32[32]{0:T(128)S(1)}, u32[32]{0:T(128)}, u32[]{:S(2)}) copy-start(u32[32]{0:T(128)} %constant.105) | copy-start | bytes 388
  16.8 6.6 %copy-start.10 = (s32[16]{0:T(128)S(1)}, s32[16]{0:T(128)}, u32[]{:S(2)}) copy-start(s32[16]{0:T(128)} %param.17) | copy-start | bytes 196
  16.8 56.8 %copy-start.8 = (s32[32]{0:T(128)S(1)}, s32[32]{0:T(128)}, u32[]{:S(2)}) copy-start(s32[32]{0:T(128)} %param.19) | copy-start | bytes 388
  16.8 59.0 %all-to-all-start = ((bf16[32,32,2048]{2,1,0:T(8,128)(2,1)}), bf16[32,32,2048]{2,1,0:T(8,128)(2,1)}, u32[]{:S(2)}, u32[]{:S(2)}) async-start(bf16[32,32,2048]{2,1,0:T(8,128)(2,1)} %broadcast_select_fusion), calls=%async_computation.1 | async-start | bytes 8388608 | tf_op jit(solution)/shard_map/all_to_all | solution.py:142
  22.1 115.9 %all-gather.8.cloned.1.call-start = ((), (), s32[]{:S(2)}) async-start(), calls=%async_computation.5 | async-start | bytes 1966080 | tf_op jit(solution)/shard_map/all_gather | solution.py:190
  75.8 4.1 %copy-start.9 = (bf16[4,192,2048]{2,1,0:T(8,128)(2,1)S(1)}, bf16[4,192,2048]{2,1,0:T(8,128)(2,1)}, u32[]{:S(2)}) copy-start(bf16[4,192,2048]{2,1,0:T(8,128)(2,1)} %param.14) | copy-start | bytes 9437188
  87.3 5.5 %copy-start.6 = (bf16[512,2048]{1,0:T(8,128)(2,1)S(1)}, bf16[512,2048]{1,0:T(8,128)(2,1)}, u32[]{:S(2)}) copy-start(bf16[512,2048]{1,0:T(8,128)(2,1)} %param.11) | copy-start | bytes 6291460
  92.0 195.2 %all-gather.6.cloned.1.call-start = ((), (), s32[]{:S(2)}) async-start(), calls=%async_computation.4 | async-start | bytes 10485760 | tf_op jit(solution)/shard_map/all_gather | solution.py:173
  92.7 238.8 %reduce-scatter.2.cloned.1.call-start = ((), (), s32[]{:S(2)}) async-start(), calls=%async_computation.3 | async-start | bytes 2621440 | tf_op jit(solution)/shard_map/reduce_scatter | solution.py:166
  97.6 1.6 copy-start.7
  147.5 184.0 %all-to-all-start.1 = ((bf16[32,32,1280]{2,1,0:T(8,128)(2,1)}), bf16[32,32,1280]{2,1,0:T(8,128)(2,1)S(1)}, u32[]{:S(2)}, u32[]{:S(2)}) async-start(bf16[32,32,1280]{2,1,0:T(8,128)(2,1)} %fusion), calls=%async_computation.2 | async-start | bytes 5242880 | tf_op jit(solution)/shard_map/all_to_all | solution.py:210
  287.2 44.3 %copy-start.3 = (f32[128,128]{1,0:T(8,128)S(1)}, f32[128,128]{1,0:T(8,128)}, u32[]{:S(2)}) copy-start(f32[128,128]{1,0:T(8,128)} %constant.98.clone.refs_5_) | copy-start | bytes 196612
  287.2 44.3 %copy-start.4 = (f32[128,128]{1,0:T(8,128)S(1)}, f32[128,128]{1,0:T(8,128)}, u32[]{:S(2)}) copy-start(f32[128,128]{1,0:T(8,128)} %constant.99.clone.refs_6_) | copy-start | bytes 196612
  287.2 44.3 %copy-start.5 = (s32[16]{0:T(128)S(1)}, s32[16]{0:T(128)}, u32[]{:S(2)}) copy-start(s32[16]{0:T(128)} %refs_1_.1) | copy-start | bytes 196
  331.6 1.6 copy-start.1
  333.2 1.0 copy-start.2
Sparse Core Ops, SparseCore 0:
  92.1 45.8 all-gather.7
  139.6 147.6 all-gather.5
  289.5 41.9 reduce-scatter.1

commit v2 on v1

v2 whole, which is shorter than its diff:
```python
import math

import jax
import jax.numpy as jnp
import numpy as np
from jax import lax
from jax.experimental import pallas as pl
from jax.experimental.pallas import tpu as pltpu
from jax.sharding import PartitionSpec as P

HEAD_SIZE = 128
HALF = HEAD_SIZE // 2
CHUNKS = 2

adapter_scale = 0.5
rope_theta = 500000.0


def rope_tables(seq_len, rows):
    frequency = np.float64(rope_theta) ** (-(np.arange(HALF, dtype=np.float64) * 2.0 / HEAD_SIZE))
    angles = (np.arange(rows) % seq_len).astype(np.float64)[:, None] * frequency[None, :]
    cosine = np.concatenate([np.cos(angles), np.cos(angles)], axis=1)
    sine = np.concatenate([-np.sin(angles), np.sin(angles)], axis=1)
    return cosine.astype(np.float32), sine.astype(np.float32)


def pick_kernel(count, wide, picks, tokens, marks, out, sems, mark_sem):
    copies = [
        pltpu.make_async_copy(tokens.at[picks[s]], out.at[s, :, pl.ds(0, wide)], sems.at[s])
        for s in range(count)
    ]
    tail = pltpu.make_async_copy(marks, out.at[:, :, pl.ds(wide, HEAD_SIZE)], mark_sem)
    for copy in copies:
        copy.start()
    tail.start()
    for copy in copies:
        copy.wait()
    tail.wait()


def pick_slots(picks, tokens, marks):
    count = picks.shape[0]
    _, seq_len, wide = tokens.shape
    anywhere = pl.BlockSpec(memory_space=pl.ANY)

    def body(*refs):
        pick_kernel(count, wide, *refs)

    return pl.pallas_call(
        body,
        out_shape=jax.ShapeDtypeStruct((count, seq_len, wide + HEAD_SIZE), tokens.dtype),
        grid_spec=pltpu.PrefetchScalarGridSpec(
            num_scalar_prefetch=1,
            grid=(1,),
            in_specs=[anywhere, anywhere],
            out_specs=anywhere,
            scratch_shapes=[pltpu.SemaphoreType.DMA((count,)), pltpu.SemaphoreType.DMA],
        ),
    )(picks, tokens, marks)


def down_project(received, down):
    rows, lanes = received.shape
    adapters, outs, wide = down.shape
    block = min(256, rows)

    def body(x, w, out):
        features = x[:, :wide]
        mark = x[:, wide : wide + 1].astype(jnp.float32)
        total = jnp.zeros((block, outs), jnp.float32)
        for a in range(adapters):
            one = lax.dot_general(
                features, w[a], (((1,), (1,)), ((), ())), preferred_element_type=jnp.float32
            )
            total = jnp.where(mark == float(a), one, total)
        out[...] = total.astype(jnp.bfloat16)

    return pl.pallas_call(
        body,
        out_shape=jax.ShapeDtypeStruct((rows, outs), jnp.bfloat16),
        grid=(rows // block,),
        in_specs=[
            pl.BlockSpec((block, lanes), lambda i: (i, 0)),
            pl.BlockSpec((adapters, outs, wide), lambda i: (0, 0, 0)),
        ],
        out_specs=pl.BlockSpec((block, outs), lambda i: (i, 0)),
        compiler_params=pltpu.CompilerParams(vmem_limit_bytes=32 << 20),
        cost_estimate=pl.CostEstimate(
            flops=2 * rows * outs * adapters * wide, bytes_accessed=9 << 20, transcendentals=0
        ),
    )(received, down)


def up_project(shrink, received, up_query, up_key, up_value):
    rows, outs = shrink.shape
    adapters, rank, query_cols = up_query.shape
    wide = received.shape[1] - HEAD_SIZE
    block = min(256, rows)
    cols = query_cols + 2 * HEAD_SIZE

    def body(low, marks, wq, wk, wv, out):
        mark = marks[:, :1].astype(jnp.float32)
        start = 0
        for side, w in enumerate((wq, wk, wv)):
            width = w.shape[2]
            part = low[:, side * rank : (side + 1) * rank].astype(jnp.float32)
            total = jnp.zeros((block, width), jnp.float32)
            for a in range(adapters):
                mine = jnp.where(mark == float(a), part, 0.0).astype(jnp.bfloat16)
                total += jnp.dot(mine, w[a], preferred_element_type=jnp.float32)
            out[:, start : start + width] = (adapter_scale * total).astype(jnp.bfloat16)
            start += width

    whole = lambda w: pl.BlockSpec(w.shape, lambda i: (0, 0, 0))
    return pl.pallas_call(
        body,
        out_shape=jax.ShapeDtypeStruct((rows, cols), jnp.bfloat16),
        grid=(rows // block,),
        in_specs=[
            pl.BlockSpec((block, outs), lambda i: (i, 0)),
            pl.BlockSpec((block, HEAD_SIZE), lambda i: (i, wide // HEAD_SIZE)),
            whole(up_query),
            whole(up_key),
            whole(up_value),
        ],
        out_specs=pl.BlockSpec((block, cols), lambda i: (i, 0)),
        compiler_params=pltpu.CompilerParams(vmem_limit_bytes=32 << 20),
        cost_estimate=pl.CostEstimate(
            flops=2 * rows * rank * adapters * cols, bytes_accessed=4 << 20, transcendentals=0
        ),
    )(shrink, received, up_query, up_key, up_value)


def attend_kernel(seq_len, per_block, heads_here, slots, lengths, base, pair, delta, cosine, sine, out):
    block = pl.program_id(0)
    rows = per_block * seq_len
    query_cols = heads_here * HEAD_SIZE
    picked = [slots[block * per_block + j] for j in range(per_block)]
    sizes = [lengths[block * per_block + j] for j in range(per_block)]

    def change(start, width):
        return jnp.concatenate(
            [delta[s, :, start : start + width] for s in picked], axis=0
        ).astype(jnp.float32)

    cos = cosine[...]
    sin = sine[...]

    def rotate(v):
        return (v * cos + pltpu.roll(v, HALF, 1) * sin).astype(jnp.bfloat16)

    sums = pair[0].astype(jnp.float32)
    for t in range(1, pair.shape[0]):
        sums += pair[t].astype(jnp.float32)
    keys_raw = (sums[:, :HEAD_SIZE] + change(query_cols, HEAD_SIZE)).astype(jnp.bfloat16)
    values = (sums[:, HEAD_SIZE:] + change(query_cols + HEAD_SIZE, HEAD_SIZE)).astype(jnp.bfloat16)
    keys = rotate(keys_raw.astype(jnp.float32))
    q_at = lax.broadcasted_iota(jnp.int32, (rows, rows), 0)
    p_at = lax.broadcasted_iota(jnp.int32, (rows, rows), 1)
    p_request = p_at // seq_len
    q_row = lax.broadcasted_iota(jnp.int32, (rows, HEAD_SIZE), 0)
    limit = jnp.zeros((rows, rows), jnp.int32)
    q_limit = jnp.zeros((rows, HEAD_SIZE), jnp.int32)
    for j in range(per_block):
        limit = jnp.where(p_request == j, sizes[j] + j * seq_len, limit)
        q_limit = jnp.where(q_row // seq_len == j, sizes[j] + j * seq_len, q_limit)
    allowed = (p_request == q_at // seq_len) & (p_at <= q_at) & (p_at < limit)
    live = q_row < q_limit
    for h in range(heads_here):
        at = h * HEAD_SIZE
        query = rotate(base[:, at : at + HEAD_SIZE] + change(at, HEAD_SIZE))
        scores = lax.dot_general(
            query, keys, (((1,), (1,)), ((), ())), preferred_element_type=jnp.float32
        ) * (1.0 / math.sqrt(HEAD_SIZE))
        scores = jnp.where(allowed, scores, jnp.float32(-1e30))
        weights = jnp.exp(scores - jnp.max(scores, axis=1, keepdims=True))
        probs = (weights / jnp.sum(weights, axis=1, keepdims=True)).astype(jnp.bfloat16)
        mixed = jnp.dot(probs, values, preferred_element_type=jnp.float32)
        out[:, at : at + HEAD_SIZE] = jnp.where(live, mixed, 0.0).astype(jnp.bfloat16)


def attend(slots, lengths, base, pair, delta, seq_len):
    tok_rows, query_cols = base.shape
    per_block = max(1, HEAD_SIZE // seq_len)
    rows = per_block * seq_len
    cosine, sine = rope_tables(seq_len, rows)
    whole = lambda shape: pl.BlockSpec(shape, lambda i, *_: (0,) * len(shape))
    part = lambda cols: pl.BlockSpec((rows, cols), lambda i, *_: (i, 0))

    def body(*refs):
        attend_kernel(seq_len, per_block, query_cols // HEAD_SIZE, *refs)

    return pl.pallas_call(
        body,
        out_shape=jax.ShapeDtypeStruct((tok_rows, query_cols), jnp.bfloat16),
        grid_spec=pltpu.PrefetchScalarGridSpec(
            num_scalar_prefetch=2,
            grid=(tok_rows // rows,),
            in_specs=[
                part(query_cols),
                pl.BlockSpec((pair.shape[0], rows, 2 * HEAD_SIZE), lambda i, *_: (0, i, 0)),
                whole(delta.shape),
                whole(cosine.shape),
                whole(sine.shape),
            ],
            out_specs=part(query_cols),
        ),
        compiler_params=pltpu.CompilerParams(vmem_limit_bytes=32 << 20),
    )(slots, lengths, base, pair, delta, jnp.asarray(cosine), jnp.asarray(sine))


def shards(
    tokens,
    query_weight,
    key_value_weight,
    adapter_down_tables,
    adapter_up_query,
    adapter_up_key_value,
    request_adapter,
    request_token_length,
    adapter_table_row,
):
    replicas = lax.axis_size("rep")
    tp_count = lax.axis_size("tp")
    tp_here = lax.axis_index("tp")
    tok_rows, feat_local = tokens.shape
    query_cols = query_weight.shape[1]
    pair_total = key_value_weight.shape[1]
    local_rows = adapter_down_tables.shape[0]
    rank = adapter_up_query.shape[1]
    requests_here = request_adapter.shape[0]
    seq_len = tok_rows // requests_here
    capacity = max(1, 2 * requests_here // replicas)
    slot_count = replicas * capacity
    kv_heads = pair_total // (2 * HEAD_SIZE)
    sharing = tp_count // kv_heads

    match = request_adapter[:, None] == jnp.arange(adapter_table_row.shape[0], dtype=jnp.int32)
    homes = jnp.sum(jnp.where(match, adapter_table_row[None, :], 0), axis=1)
    owners = homes // local_rows
    pos = jnp.arange(requests_here, dtype=jnp.int32)
    earlier = (owners[:, None] == owners[None, :]) & (pos[None, :] < pos[:, None])
    slot_ids = owners * capacity + jnp.sum(earlier.astype(jnp.int32), axis=1)
    slot_at = jnp.arange(slot_count, dtype=jnp.int32)
    taken = slot_ids[None, :] == slot_at[:, None]
    picks = jnp.sum(jnp.where(taken, pos, 0), axis=1)
    slot_local = jnp.sum(jnp.where(taken, (homes % local_rows)[None, :], 0), axis=1)
    marks = jnp.broadcast_to(
        slot_local.astype(jnp.bfloat16)[:, None, None], (slot_count, seq_len, HEAD_SIZE)
    )

    send = pick_slots(picks, tokens.reshape(requests_here, seq_len, feat_local), marks)
    received = lax.all_to_all(send, "rep", split_axis=0, concat_axis=0, tiled=True)
    received = received.reshape(slot_count * seq_len, feat_local + HEAD_SIZE)

    base_pair = jnp.dot(tokens, key_value_weight, preferred_element_type=jnp.float32)
    base_pair = base_pair.astype(jnp.bfloat16)
    side = kv_heads * HEAD_SIZE
    portion = adapter_up_key_value.shape[2]
    flat_up = adapter_up_key_value.reshape(local_rows * rank, portion)
    fold = local_rows * rank // 2
    pieces = []
    for t in range(tp_count):
        at = (t // sharing) * HEAD_SIZE
        up = flat_up[:, at % portion : at % portion + HEAD_SIZE]
        pieces.append(
            jnp.concatenate(
                [
                    jnp.concatenate([base_pair[:, at : at + HEAD_SIZE], up[:fold]], axis=0),
                    jnp.concatenate(
                        [base_pair[:, side + at : side + at + HEAD_SIZE], up[fold:]], axis=0
                    ),
                ],
                axis=1,
            )
        )
    swapped = lax.all_to_all(jnp.stack(pieces), "tp", split_axis=0, concat_axis=0, tiled=True)
    head = tp_here // sharing

    def up_of(column):
        both = lax.dynamic_index_in_dim(swapped, column // portion, 0, keepdims=False)[tok_rows:]
        both = jnp.concatenate([both[:, :HEAD_SIZE], both[:, HEAD_SIZE:]], axis=0)
        return both.reshape(local_rows, rank, HEAD_SIZE)

    up_key = up_of(head * HEAD_SIZE)
    up_value = up_of(side + head * HEAD_SIZE)

    chunk_rows = tok_rows // CHUNKS
    weight = query_weight.reshape(tp_count, feat_local, query_cols)
    bases = []
    for c in range(CHUNKS):
        gathered = lax.all_gather(
            tokens[c * chunk_rows : (c + 1) * chunk_rows], "tp", axis=0, tiled=False
        )
        bases.append(
            jnp.einsum("tnf,tfc->nc", gathered, weight, preferred_element_type=jnp.float32)
        )
    base_query = jnp.concatenate(bases, axis=0)

    partial = down_project(received, adapter_down_tables)
    partial = partial.reshape(tp_count, slot_count * seq_len // tp_count, 3 * rank)
    parts = lax.all_to_all(partial, "tp", split_axis=0, concat_axis=0, tiled=True)
    total = parts[0].astype(jnp.float32)
    for t in range(1, tp_count):
        total = total + parts[t].astype(jnp.float32)
    own = jnp.broadcast_to(total.astype(jnp.bfloat16)[None], partial.shape)
    shrink = lax.all_to_all(own, "tp", split_axis=0, concat_axis=0, tiled=True)
    shrink = shrink.reshape(slot_count * seq_len, 3 * rank)

    delta = up_project(shrink, received, adapter_up_query, up_key, up_value)
    returned = lax.all_to_all(
        delta.reshape(slot_count, seq_len, delta.shape[1]),
        "rep",
        split_axis=0,
        concat_axis=0,
        tiled=True,
    )
    return attend(slot_ids, request_token_length, base_query, swapped, returned, seq_len)


def solution(mesh):
    placed = (
        P("rep", "tp"),
        P(None, "tp"),
        P("tp", None),
        P("rep", None, "tp"),
        P("rep", None, "tp"),
        P("rep", None, "tp"),
        P("rep"),
        P("rep"),
        P(),
    )
    return jax.shard_map(
        shards, mesh=mesh, in_specs=placed, out_specs=P("rep", "tp"), check_vma=False
    )
```

time: 354 us -> 363 us (1.025)
  Pallas kernels: 12.7 us -> 162 us
  blocking collectives: 73.6 us -> 0 us
  waiting for transfers between devices: 180 us -> 124 us
  starting transfers between devices: 9.07 us -> 22 us
  matrix products: 37.8 us -> 26.6 us
  other arithmetic: 13 us -> 3.94 us
    all_gather x2, waiting for transfers between devices: 151 us -> 0.01 us  [shards(): lax.all_gather(tokens[c * chunk_rows:(c + 1) * chunk_rows], 'tp', axis=0,...]
    pallas_call x0 -> x3, Pallas kernels: none -> 149 us  [the longest x1 137 us: pick_slots(): pl.pallas_call(body, out_shape=jax.ShapeDtypeStruct((count, seq_len, wide...]
    all_to_all x0 -> x3, waiting for transfers between devices: none -> 69.3 us  [the longest x1 46.3 us: shards(): lax.all_to_all(jnp.stack(pieces), 'tp', split_axis=0, concat_axis=0, tile...]
    unnamed x1 -> x0, blocking collectives: 49.8 us -> none
    all_to_all x1, waiting for transfers between devices: 0.01 us -> 45.1 us  [shards(): lax.all_to_all(send, 'rep', split_axis=0, concat_axis=0, tiled=True)]
    reduce_scatter x1 -> x0, waiting for transfers between devices: 28.5 us -> none  [shards(): lax.psum_scatter(jnp.stack(pieces), 'tp', scatter_dimension=0, tiled=False)]
    all_gather x1 -> x0, blocking collectives: 23.8 us -> none  [shards(): up_all = lax.all_gather(adapter_up_key_value, 'tp', axis=2, tiled=True)]
    all_to_all x0 -> x3, starting transfers between devices: none -> 12.6 us  [the longest x1 5.64 us: shards(): lax.all_to_all(jnp.stack(pieces), 'tp', split_axis=0, concat_axis=0, tile...]
  transfers between devices with their start and end apart: 5 -> 7, of which waited for: 3 -> 5; matrix products, arithmetic and copies ran while one was open for 10% -> 9% of each run, Pallas kernels for 0% -> 41%
where the time goes in v2:
time: 363 us
  Pallas kernels  162 us (45%)
  waiting for transfers between devices  124 us (34%)
  matrix products  26.6 us (7%)
  starting transfers between devices  22 us (6%)
  between operations  13.7 us (4%)
  local copies, waits for them, and re-layouts  11.1 us (3%)
  other arithmetic  3.94 us (1%)
    pallas_call x1, Pallas kernels, pick_slots(): pl.pallas_call(body, out_shape=jax.ShapeDtypeStruct((count, seq_len, wide...  137 us
    all_to_all x1, waiting for transfers between devices, shards(): lax.all_to_all(jnp.stack(pieces), 'tp', split_axis=0, concat_axis=0, tile...  46.3 us
    all_to_all x1, waiting for transfers between devices, shards(): lax.all_to_all(send, 'rep', split_axis=0, concat_axis=0, tiled=True)  45.1 us
    dot_general x2, matrix products, shards(): jnp.einsum('tnf,tfc->nc', gathered, weight, preferred_element_type=jnp.fl...  22 us
    pallas_call x1, Pallas kernels, attend(): pl.pallas_call(body, out_shape=jax.ShapeDtypeStruct((tok_rows, query_cols...  12.9 us
    all_to_all x1, waiting for transfers between devices, shards(): lax.all_to_all(partial, 'tp', split_axis=0, concat_axis=0, tiled=True)  11.9 us
    all_to_all x1, waiting for transfers between devices, shards(): shrink = lax.all_to_all(own, 'tp', split_axis=0, concat_axis=0, tiled=True)  11.1 us
    all_to_all x1, waiting for transfers between devices, shards(): lax.all_to_all(delta.reshape(slot_count, seq_len, delta.shape[1]), 'rep',...  8.67 us
  transfers between devices with their start and end apart: 7, of which 5 were waited for; matrix products, arithmetic and copies ran while one was open for 9% of the time, Pallas kernels for 41%

profile of v2, /device:TPU:0, one launch (start us, length us, event | category | flops | bytes accessed | tf_op | source)
XLA Modules:
  0.0 362.6 jit_solution(17576007759963389407)
XLA Ops:
  6.5 3.1 fusion.10
  11.5 137.1 %shard_map.109 = bf16[32,32,2176]{2,1,0:T(8,128)(2,1)} custom-call(s32[32]{0:T(128)} %get-tuple-element.6.refs_0_, bf16[16,32,2048]{2,1,0:T(8,128)(2,1)} %bitcast.39, bf16[32,32,128]{2,1,0:T(8,128)(2,1)} %broadcast_in_dim.59.refs_2_), custom_call_target="tpu_custom_call" | custom-call | tf_op jit(solution)/shard_map/pallas_call | solution.py:49
  148.6 5.3 %all-to-all-start.1 = ((bf16[32,32,2176]{2,1,0:T(8,128)(2,1)}), bf16[32,32,2176]{2,1,0:T(8,128)(2,1)}, u32[]{:S(2)}, u32[]{:S(2)}) async-start(bf16[32,32,2176]{2,1,0:T(8,128)(2,1)} %shard_map.109), calls=%async_computation.1 | async-start | bytes 8912896 | tf_op jit(solution)/shard_map/all_to_all | solution.py:253
  154.8 4.5 %convolution_convert_fusion = bf16[512,1024]{1,0:T(8,128)(2,1)S(1)} fusion(bf16[512,2048]{1,0:T(8,128)(2,1)S(1)} %copy-done.8, bf16[2048,1024]{1,0:T(8,128)(2,1)} %param.13), kind=kOutput, calls=%fused_computation.1 | convolution fusion | flops 2148007936 | bytes 7340032 | tf_op jit(solution)/shard_map/dot_general | solution.py:256
  159.6 1.3 pad_maximum_fusion.1
  160.9 45.1 %all-to-all-done.1 = bf16[32,32,2176]{2,1,0:T(8,128)(2,1)} async-done(((bf16[32,32,2176]{2,1,0:T(8,128)(2,1)}), bf16[32,32,2176]{2,1,0:T(8,128)(2,1)}, u32[]{:S(2)}, u32[]{:S(2)}) %all-to-all-start.1) | async-done | bytes 4456480 | tf_op jit(solution)/shard_map/all_to_all | solution.py:253
  206.0 5.6 %all-to-all-start = ((bf16[4,640,256]{2,1,0:T(8,128)(2,1)}), bf16[4,640,256]{2,1,0:T(8,128)(2,1)S(1)}, u32[]{:S(2)}, u32[]{:S(2)}) async-start(bf16[4,640,256]{2,1,0:T(8,128)(2,1)} %pad_maximum_fusion.1), calls=%async_computation | async-start | bytes 2621440 | tf_op jit(solution)/shard_map/all_to_all | solution.py:277
  211.6 1.9 copy-done.7
  213.6 6.4 %shard_map.110 = bf16[1024,192]{1,0:T(8,128)(2,1)S(1)} custom-call(bf16[1024,2176]{1,0:T(8,128)(2,1)} %bitcast.11.x.marks, bf16[4,192,2048]{2,1,0:T(8,128)(2,1)S(1)} %copy-done.7), custom_call_target="tpu_custom_call" | custom-call | flops 3221225472 | bytes 9437184 | tf_op jit(solution)/shard_map/pallas_call | solution.py:78
  219.9 1.0 copy.14
  220.9 46.3 %all-to-all-done.refs_3_ = bf16[4,640,256]{2,1,0:T(8,128)(2,1)S(1)} async-done(((bf16[4,640,256]{2,1,0:T(8,128)(2,1)}), bf16[4,640,256]{2,1,0:T(8,128)(2,1)S(1)}, u32[]{:S(2)}, u32[]{:S(2)}) %all-to-all-start) | async-done | bytes 1310752 | tf_op jit(solution)/shard_map/all_to_all | solution.py:277
  267.2 3.5 all-to-all-start.2
  270.8 11.9 %all-to-all-done.2 = bf16[4,256,192]{1,2,0:T(8,128)(2,1)S(1)} async-done(((bf16[4,256,192]{1,2,0:T(8,128)(2,1)}), bf16[4,256,192]{1,2,0:T(8,128)(2,1)S(1)}, u32[]{:S(2)}, u32[]{:S(2)}) %all-to-all-start.2) | async-done | bytes 393248 | tf_op jit(solution)/shard_map/all_to_all | solution.py:302
  283.5 3.5 all-to-all-start.3
  287.0 11.1 %all-to-all-done.3 = bf16[4,256,192]{1,2,0:T(8,128)(2,1)S(1)} async-done(((bf16[4,256,192]{1,2,0:T(8,128)(2,1)}), bf16[4,256,192]{1,2,0:T(8,128)(2,1)S(1)}, u32[]{:S(2)}, u32[]{:S(2)}) %all-to-all-start.3) | async-done | bytes 393248 | tf_op jit(solution)/shard_map/all_to_all | solution.py:307
  298.4 5.3 %shard_map.111 = bf16[1024,1280]{1,0:T(8,128)(2,1)} custom-call(bf16[1024,192]{1,0:T(8,128)(2,1)S(1)} %bitcast.35, bf16[1024,2176]{1,0:T(8,128)(2,1)} %bitcast.11.x.marks, bf16[4,64,1024]{2,1,0:T(8,128)(2,1)S(1)} %copy-done.3, bf16[4,64,128]{2,1,0:T(8,128)(2,1)S(1)} %bitcast.38, bf16[4,64,128]{2,1,0:T(8,128)(2,1)S(1)} %bitcast.37), custom_call_target="tpu_custom_call" | custom-call | flops 671088640 | bytes 4194304 | tf_op jit(solution)/shard_map/pallas_call | solution.py:115
  303.7 4.0 %all-to-all-start.4 = ((bf16[32,32,1280]{2,1,0:T(8,128)(2,1)}), bf16[32,32,1280]{2,1,0:T(8,128)(2,1)S(1)}, u32[]{:S(2)}, u32[]{:S(2)}) async-start(bf16[32,32,1280]{2,1,0:T(8,128)(2,1)} %bitcast.19), calls=%async_computation.4 | async-start | bytes 5242880 | tf_op jit(solution)/shard_map/all_to_all | solution.py:311
  307.7 12.6 %convolution_bitcast_fusion = f32[256,1024]{1,0:T(8,128)} fusion(bf16[4,256,2048]{2,1,0:T(8,128)(2,1)} %bitcast.43, bf16[4,2048,1024]{2,1,0:T(8,128)(2,1)} %bitcast.41), kind=kOutput, calls=%fused_computation.2 | convolution fusion | flops 4294967296 | bytes 22020096 | tf_op jit(solution)/shard_map/tnf,tfc->nc/dot_general | solution.py:296
  320.3 9.5 %convolution_bitcast_fusion.1 = f32[256,1024]{1,0:T(8,128)S(1)} fusion(bf16[4,256,2048]{2,1,0:T(8,128)(2,1)} %bitcast.44, bf16[4,2048,1024]{2,1,0:T(8,128)(2,1)} %bitcast.42), kind=kOutput, calls=%fused_computation.3 | convolution fusion | flops 4294967296 | bytes 22020096 | tf_op jit(solution)/shard_map/tnf,tfc->nc/dot_general | solution.py:296
  329.9 1.5 pad_maximum_fusion.refs_2_
  331.3 8.7 %all-to-all-done.4.refs_4_ = bf16[32,32,1280]{2,1,0:T(8,128)(2,1)S(1)} async-done(((bf16[32,32,1280]{2,1,0:T(8,128)(2,1)}), bf16[32,32,1280]{2,1,0:T(8,128)(2,1)S(1)}, u32[]{:S(2)}, u32[]{:S(2)}) %all-to-all-start.4) | async-done | bytes 2621472 | tf_op jit(solution)/shard_map/all_to_all | solution.py:311
  340.0 1.6 copy-done
  341.6 1.3 copy-done.2
  342.9 12.9 %shard_map.112 = bf16[512,1024]{1,0:T(8,128)(2,1)} custom-call(s32[16]{0:T(128)S(1)} %multiply_add_fusion.refs_0_, s32[16]{0:T(128)S(1)} %copy-done.6, f32[512,1024]{1,0:T(8,128)S(1)} %copy-done, bf16[4,640,256]{2,1,0:T(8,128)(2,1)S(1)} %copy-done.2, bf16[32,32,1280]{2,1,0:T(8,128)(2,1)S(1)} %all-to-all-done.4.refs_4_, f32[128,128]{1,0:T(8,128)S(1)} %copy-done.4, ...), custom_call_target="tpu_custom_call" | custom-call | tf_op jit(solution)/shard_map/pallas_call | solution.py:193
  (47 shorter events, 4.1 us)
Async XLA Ops:
  6.5 3.2 copy-start.12
  6.5 3.2 copy-start.11
  6.5 301.2 %all-gather.7.cloned.1.call-start = ((), (), s32[]{:S(2)}) async-start(), calls=%async_computation.6 | async-start | bytes 5242880 | tf_op jit(solution)/shard_map/all_gather | solution.py:292
  148.6 6.1 %copy-start.10 = (bf16[4,64,256]{2,1,0:T(8,128)(2,1)S(1)}, bf16[4,64,256]{2,1,0:T(8,128)(2,1)}, u32[]{:S(2)}) copy-start(bf16[4,64,256]{2,1,0:T(8,128)(2,1)} %param.16) | copy-start | bytes 393220
  148.6 6.1 %copy-start.8 = (bf16[512,2048]{1,0:T(8,128)(2,1)S(1)}, bf16[512,2048]{1,0:T(8,128)(2,1)}, u32[]{:S(2)}) copy-start(bf16[512,2048]{1,0:T(8,128)(2,1)} %param.11) | copy-start | bytes 6291460
  148.6 57.3 %all-to-all-start.1 = ((bf16[32,32,2176]{2,1,0:T(8,128)(2,1)}), bf16[32,32,2176]{2,1,0:T(8,128)(2,1)}, u32[]{:S(2)}, u32[]{:S(2)}) async-start(bf16[32,32,2176]{2,1,0:T(8,128)(2,1)} %shard_map.109), calls=%async_computation.1 | async-start | bytes 8912896 | tf_op jit(solution)/shard_map/all_to_all | solution.py:253
  154.0 166.3 %all-gather.5.cloned.1.call-start = ((), (), s32[]{:S(2)}) async-start(), calls=%async_computation.5 | async-start | bytes 5242880 | tf_op jit(solution)/shard_map/all_gather | solution.py:292
  206.0 61.2 %all-to-all-start = ((bf16[4,640,256]{2,1,0:T(8,128)(2,1)}), bf16[4,640,256]{2,1,0:T(8,128)(2,1)S(1)}, u32[]{:S(2)}, u32[]{:S(2)}) async-start(bf16[4,640,256]{2,1,0:T(8,128)(2,1)} %pad_maximum_fusion.1), calls=%async_computation | async-start | bytes 2621440 | tf_op jit(solution)/shard_map/all_to_all | solution.py:277
  211.6 1.9 copy-start.7
  219.9 78.4 %copy-start.3 = (bf16[4,64,1024]{2,1,0:T(8,128)(2,1)S(1)}, bf16[4,64,1024]{2,1,0:T(8,128)(2,1)}, u32[]{:S(2)}) copy-start(bf16[4,64,1024]{2,1,0:T(8,128)(2,1)} %wq.1) | copy-start | bytes 1572868
  267.2 36.4 %copy-start.1 = (bf16[4,640,256]{2,1,0:T(8,128)(2,1)}, bf16[4,640,256]{2,1,0:T(8,128)(2,1)S(1)}, u32[]{:S(2)}) copy-start(bf16[4,640,256]{2,1,0:T(8,128)(2,1)S(1)} %all-to-all-done.refs_3_) | copy-start | bytes 3932164
  267.2 15.4 %all-to-all-start.2 = ((bf16[4,256,192]{1,2,0:T(8,128)(2,1)}), bf16[4,256,192]{1,2,0:T(8,128)(2,1)S(1)}, u32[]{:S(2)}, u32[]{:S(2)}) async-start(bf16[4,256,192]{1,2,0:T(8,128)(2,1)} %copy.14), calls=%async_computation.2 | async-start | bytes 786432 | tf_op jit(solution)/shard_map/all_to_all | solution.py:302
  283.5 14.7 %all-to-all-start.3 = ((bf16[4,256,192]{1,2,0:T(8,128)(2,1)}), bf16[4,256,192]{1,2,0:T(8,128)(2,1)S(1)}, u32[]{:S(2)}, u32[]{:S(2)}) async-start(bf16[4,256,192]{1,2,0:T(8,128)(2,1)} %broadcast_in_dim.61), calls=%async_computation.3 | async-start | bytes 786432 | tf_op jit(solution)/shard_map/all_to_all | solution.py:307
  303.7 36.3 %all-to-all-start.4 = ((bf16[32,32,1280]{2,1,0:T(8,128)(2,1)}), bf16[32,32,1280]{2,1,0:T(8,128)(2,1)S(1)}, u32[]{:S(2)}, u32[]{:S(2)}) async-start(bf16[32,32,1280]{2,1,0:T(8,128)(2,1)} %bitcast.19), calls=%async_computation.4 | async-start | bytes 5242880 | tf_op jit(solution)/shard_map/all_to_all | solution.py:311
  320.3 9.5 %copy-start.9 = (f32[256,1024]{1,0:T(8,128)S(1)}, f32[256,1024]{1,0:T(8,128)}, u32[]{:S(2)}) copy-start(f32[256,1024]{1,0:T(8,128)} %convolution_bitcast_fusion) | copy-start | bytes 3145732
  329.8 10.2 %copy-start.4 = (f32[128,128]{1,0:T(8,128)S(1)}, f32[128,128]{1,0:T(8,128)}, u32[]{:S(2)}) copy-start(f32[128,128]{1,0:T(8,128)} %constant.77.clone.refs_5_) | copy-start | bytes 196612
  329.8 10.2 %copy-start.5 = (f32[128,128]{1,0:T(8,128)S(1)}, f32[128,128]{1,0:T(8,128)}, u32[]{:S(2)}) copy-start(f32[128,128]{1,0:T(8,128)} %constant.78.clone.refs_6_) | copy-start | bytes 196612
  329.8 10.2 %copy-start.6 = (s32[16]{0:T(128)S(1)}, s32[16]{0:T(128)}, u32[]{:S(2)}) copy-start(s32[16]{0:T(128)} %refs_1_.1) | copy-start | bytes 196
  340.0 1.6 copy-start
  341.6 1.3 copy-start.2
Sparse Core Ops, SparseCore 0:
  9.8 83.4 all-gather.6
  156.4 110.6 all-gather.4

commit v3 on v2

--- a/solution.py
+++ b/solution.py
@@ -10,7 +10,6 @@
 
 HEAD_SIZE = 128
 HALF = HEAD_SIZE // 2
-CHUNKS = 2
 
 adapter_scale = 0.5
 rope_theta = 500000.0
@@ -24,39 +23,29 @@
     return cosine.astype(np.float32), sine.astype(np.float32)
 
 
-def pick_kernel(count, wide, picks, tokens, marks, out, sems, mark_sem):
-    copies = [
-        pltpu.make_async_copy(tokens.at[picks[s]], out.at[s, :, pl.ds(0, wide)], sems.at[s])
-        for s in range(count)
-    ]
-    tail = pltpu.make_async_copy(marks, out.at[:, :, pl.ds(wide, HEAD_SIZE)], mark_sem)
-    for copy in copies:
-        copy.start()
-    tail.start()
-    for copy in copies:
-        copy.wait()
-    tail.wait()
-
-
-def pick_slots(picks, tokens, marks):
+def pick_slots(picks, marks, tokens):
     count = picks.shape[0]
     _, seq_len, wide = tokens.shape
-    anywhere = pl.BlockSpec(memory_space=pl.ANY)
-
-    def body(*refs):
-        pick_kernel(count, wide, *refs)
+    group = min(4, count)
+
+    def body(pick, mark, x, out):
+        first = pl.program_id(0) * group
+        for j in range(group):
+            out[j, :, :wide] = x[pick[first + j]]
+            value = mark[first + j].astype(jnp.float32)
+            out[j, :, wide:] = jnp.full((seq_len, HEAD_SIZE), value, jnp.float32).astype(out.dtype)
 
     return pl.pallas_call(
         body,
         out_shape=jax.ShapeDtypeStruct((count, seq_len, wide + HEAD_SIZE), tokens.dtype),
         grid_spec=pltpu.PrefetchScalarGridSpec(
-            num_scalar_prefetch=1,
-            grid=(1,),
-            in_specs=[anywhere, anywhere],
-            out_specs=anywhere,
-            scratch_shapes=[pltpu.SemaphoreType.DMA((count,)), pltpu.SemaphoreType.DMA],
-        ),
-    )(picks, tokens, marks)
+            num_scalar_prefetch=2,
+            grid=(count // group,),
+            in_specs=[pl.BlockSpec(tokens.shape, lambda i, *_: (0, 0, 0))],
+            out_specs=pl.BlockSpec((group, seq_len, wide + HEAD_SIZE), lambda i, *_: (i, 0, 0)),
+        ),
+        compiler_params=pltpu.CompilerParams(vmem_limit_bytes=32 << 20),
+    )(picks, marks, tokens)
 
 
 def down_project(received, down):
@@ -131,8 +120,10 @@
     )(shrink, received, up_query, up_key, up_value)
 
 
-def attend_kernel(seq_len, per_block, heads_here, slots, lengths, base, pair, delta, cosine, sine, out):
-    block = pl.program_id(0)
+def attend_kernel(
+    seq_len, per_block, heads_here, first, slots, lengths, base, pair, delta, cosine, sine, out
+):
+    block = first + pl.program_id(0)
     rows = per_block * seq_len
     query_cols = heads_here * HEAD_SIZE
     picked = [slots[block * per_block + j] for j in range(per_block)]
@@ -179,34 +170,45 @@
         out[:, at : at + HEAD_SIZE] = jnp.where(live, mixed, 0.0).astype(jnp.bfloat16)
 
 
-def attend(slots, lengths, base, pair, delta, seq_len):
-    tok_rows, query_cols = base.shape
+def attend(slots, lengths, base, pair, delta, seq_len, start, tok_rows, earlier):
+    base_rows, query_cols = base.shape
     per_block = max(1, HEAD_SIZE // seq_len)
     rows = per_block * seq_len
+    first = start // rows
     cosine, sine = rope_tables(seq_len, rows)
     whole = lambda shape: pl.BlockSpec(shape, lambda i, *_: (0,) * len(shape))
-    part = lambda cols: pl.BlockSpec((rows, cols), lambda i, *_: (i, 0))
+    carried = [] if earlier is None else [earlier]
 
     def body(*refs):
-        attend_kernel(seq_len, per_block, query_cols // HEAD_SIZE, *refs)
+        kept = refs[:7] + refs[7 + len(carried) :]
+        attend_kernel(seq_len, per_block, query_cols // HEAD_SIZE, first, *kept)
 
     return pl.pallas_call(
         body,
         out_shape=jax.ShapeDtypeStruct((tok_rows, query_cols), jnp.bfloat16),
         grid_spec=pltpu.PrefetchScalarGridSpec(
             num_scalar_prefetch=2,
-            grid=(tok_rows // rows,),
+            grid=(base_rows // rows,),
             in_specs=[
-                part(query_cols),
-                pl.BlockSpec((pair.shape[0], rows, 2 * HEAD_SIZE), lambda i, *_: (0, i, 0)),
+                pl.BlockSpec((rows, query_cols), lambda i, *_: (i, 0)),
+                pl.BlockSpec(
+                    (pair.shape[0], rows, 2 * HEAD_SIZE), lambda i, *_: (0, first + i, 0)
+                ),
                 whole(delta.shape),
                 whole(cosine.shape),
                 whole(sine.shape),
-            ],
-            out_specs=part(query_cols),
-        ),
+            ]
+            + [pl.BlockSpec(memory_space=pl.ANY)] * len(carried),
+            out_specs=pl.BlockSpec((rows, query_cols), lambda i, *_: (first + i, 0)),
+        ),
+        input_output_aliases={7: 0} if carried else {},
         compiler_params=pltpu.CompilerParams(vmem_limit_bytes=32 << 20),
-    )(slots, lengths, base, pair, delta, jnp.asarray(cosine), jnp.asarray(sine))
+        cost_estimate=pl.CostEstimate(
+            flops=4 * base_rows * rows * query_cols,
+            bytes_accessed=6 * base_rows * query_cols,
+            transcendentals=base_rows * query_cols,
+        ),
+    )(slots, lengths, base, pair, delta, jnp.asarray(cosine), jnp.asarray(sine), *carried)
 
 
 def shards(
@@ -245,11 +247,8 @@
     taken = slot_ids[None, :] == slot_at[:, None]
     picks = jnp.sum(jnp.where(taken, pos, 0), axis=1)
     slot_local = jnp.sum(jnp.where(taken, (homes % local_rows)[None, :], 0), axis=1)
-    marks = jnp.broadcast_to(
-        slot_local.astype(jnp.bfloat16)[:, None, None], (slot_count, seq_len, HEAD_SIZE)
-    )
-
-    send = pick_slots(picks, tokens.reshape(requests_here, seq_len, feat_local), marks)
+
+    send = pick_slots(picks, slot_local, tokens.reshape(requests_here, seq_len, feat_local))
     received = lax.all_to_all(send, "rep", split_axis=0, concat_axis=0, tiled=True)
     received = received.reshape(slot_count * seq_len, feat_local + HEAD_SIZE)
 
@@ -285,17 +284,15 @@
     up_key = up_of(head * HEAD_SIZE)
     up_value = up_of(side + head * HEAD_SIZE)
 
-    chunk_rows = tok_rows // CHUNKS
+    early = tok_rows * 3 // 4
     weight = query_weight.reshape(tp_count, feat_local, query_cols)
-    bases = []
-    for c in range(CHUNKS):
-        gathered = lax.all_gather(
-            tokens[c * chunk_rows : (c + 1) * chunk_rows], "tp", axis=0, tiled=False
-        )
-        bases.append(
-            jnp.einsum("tnf,tfc->nc", gathered, weight, preferred_element_type=jnp.float32)
-        )
-    base_query = jnp.concatenate(bases, axis=0)
+
+    def project(gathered):
+        return jnp.einsum("tnf,tfc->nc", gathered, weight, preferred_element_type=jnp.float32)
+
+    first = lax.all_gather(tokens[:early], "tp", axis=0, tiled=False)
+    late_rows, received = lax.optimization_barrier((tokens[early:], received))
+    second = lax.all_gather(late_rows, "tp", axis=0, tiled=False)
 
     partial = down_project(received, adapter_down_tables)
     partial = partial.reshape(tp_count, slot_count * seq_len // tp_count, 3 * rank)
@@ -315,7 +312,10 @@
         concat_axis=0,
         tiled=True,
     )
-    return attend(slot_ids, request_token_length, base_query, swapped, returned, seq_len)
+    fixed = (swapped, returned, seq_len)
+    out = attend(slot_ids, request_token_length, project(first), *fixed, 0, tok_rows, None)
+    second, out = lax.optimization_barrier((second, out))
+    return attend(slot_ids, request_token_length, project(second), *fixed, early, tok_rows, out)
 
 
 def solution(mesh):

time: 363 us -> 254 us (0.70)
  Pallas kernels: 162 us -> 26 us
  waiting for transfers between devices: 124 us -> 142 us
  starting transfers between devices: 22 us -> 27.9 us
    pallas_call x1, Pallas kernels: 137 us -> 0.98 us  [pick_slots(): pl.pallas_call(body, out_shape=jax.ShapeDtypeStruct((count, seq_len, wide...]
    all_to_all x1, waiting for transfers between devices: 8.67 us -> 19.1 us  [shards(): lax.all_to_all(delta.reshape(slot_count, seq_len, delta.shape[1]), 'rep',...]
    all_to_all x1, waiting for transfers between devices: 46.3 us -> 53.6 us  [shards(): lax.all_to_all(jnp.stack(pieces), 'tp', split_axis=0, concat_axis=0, tile...]
    unnamed x26 -> x30, local copies, waits for them, and re-layouts: 4.87 us -> 8.29 us
    pallas_call x1 -> x2, Pallas kernels: 12.9 us -> 14.1 us  [attend(): pl.pallas_call(body, out_shape=jax.ShapeDtypeStruct((tok_rows, query_cols...]
  transfers between devices with their start and end apart: 7 -> 7, of which waited for: 5 -> 5; matrix products, arithmetic and copies ran while one was open for 9% -> 9% of each run, Pallas kernels for 41% -> 9%
where the time goes in v3:
time: 254 us; the launch traced here: 253 us
  waiting for transfers between devices  142 us (56%)
  starting transfers between devices  27.9 us (11%)
  matrix products  27 us (11%)
  Pallas kernels  26 us (10%)
  local copies, waits for them, and re-layouts  14.2 us (6%)
  between operations  13.6 us (5%)
    all_to_all x1, waiting for transfers between devices, shards(): lax.all_to_all(jnp.stack(pieces), 'tp', split_axis=0, concat_axis=0, tile...  53.6 us
    all_to_all x1, waiting for transfers between devices, shards(): lax.all_to_all(send, 'rep', split_axis=0, concat_axis=0, tiled=True)  45.3 us
    dot_general x2, matrix products, project(): jnp.einsum('tnf,tfc->nc', gathered, weight, preferred_element_type=jnp.fl...  21.9 us
    all_to_all x1, waiting for transfers between devices, shards(): lax.all_to_all(delta.reshape(slot_count, seq_len, delta.shape[1]), 'rep',...  19.1 us
    pallas_call x2, Pallas kernels, attend(): pl.pallas_call(body, out_shape=jax.ShapeDtypeStruct((tok_rows, query_cols...  14.1 us
    all_to_all x1, waiting for transfers between devices, shards(): lax.all_to_all(partial, 'tp', split_axis=0, concat_axis=0, tiled=True)  13.8 us
    all_to_all x1, waiting for transfers between devices, shards(): shrink = lax.all_to_all(own, 'tp', split_axis=0, concat_axis=0, tiled=True)  9.67 us
    unnamed x30, local copies, waits for them, and re-layouts  8.29 us
  transfers between devices with their start and end apart: 7, of which 5 were waited for; matrix products, arithmetic and copies ran while one was open for 9% of the time, Pallas kernels for 9%

profile of v3, /device:TPU:0, one launch (start us, length us, event | category | flops | bytes accessed | tf_op | source)
XLA Modules:
  0.0 252.8 jit_solution(12762159777464684249)
XLA Ops:
  6.5 2.9 %slice.91 = bf16[384,2048]{1,0:T(8,128)(2,1)} slice(bf16[512,2048]{1,0:T(8,128)(2,1)} %param.13), slice={[0:384], [0:2048]} | slice | bytes 3145728 | tf_op jit(solution)/shard_map/slice | solution.py:293
  11.0 2.1 copy-done
  13.1 5.3 %all-to-all-start = ((bf16[32,32,2176]{2,1,0:T(8,128)(2,1)}), bf16[32,32,2176]{2,1,0:T(8,128)(2,1)}, u32[]{:S(2)}, u32[]{:S(2)}) async-start(bf16[32,32,2176]{2,1,0:T(8,128)(2,1)} %copy-done), calls=%async_computation | async-start | bytes 8912896 | tf_op jit(solution)/shard_map/all_to_all | solution.py:252
  18.4 5.1 %convolution_convert_fusion = bf16[512,1024]{1,0:T(8,128)(2,1)S(1)} fusion(bf16[512,2048]{1,0:T(8,128)(2,1)S(1)} %copy-done.5, bf16[2048,1024]{1,0:T(8,128)(2,1)} %param.15), kind=kOutput, calls=%fused_computation.1 | convolution fusion | flops 2148007936 | bytes 7340032 | tf_op jit(solution)/shard_map/dot_general | solution.py:255
  23.8 1.2 pad_maximum_fusion
  25.1 45.3 %all-to-all-done = bf16[32,32,2176]{2,1,0:T(8,128)(2,1)} async-done(((bf16[32,32,2176]{2,1,0:T(8,128)(2,1)}), bf16[32,32,2176]{2,1,0:T(8,128)(2,1)}, u32[]{:S(2)}, u32[]{:S(2)}) %all-to-all-start) | async-done | bytes 4456480 | tf_op jit(solution)/shard_map/all_to_all | solution.py:252
  70.4 5.6 %all-to-all-start.1 = ((bf16[4,640,256]{2,1,0:T(8,128)(2,1)}), bf16[4,640,256]{2,1,0:T(8,128)(2,1)S(1)}, u32[]{:S(2)}, u32[]{:S(2)}) async-start(bf16[4,640,256]{2,1,0:T(8,128)(2,1)} %pad_maximum_fusion), calls=%async_computation.1 | async-start | bytes 2621440 | tf_op jit(solution)/shard_map/all_to_all | solution.py:276
  76.9 1.9 copy-done.11
  78.8 6.4 %shard_map.128 = bf16[1024,192]{1,0:T(8,128)(2,1)S(1)} custom-call(bf16[1024,2176]{1,0:T(8,128)(2,1)} %bitcast.1.x.marks, bf16[4,192,2048]{2,1,0:T(8,128)(2,1)S(1)} %copy-done.11), custom_call_target="tpu_custom_call" | custom-call | flops 3221225472 | bytes 9437184 | tf_op jit(solution)/shard_map/pallas_call | solution.py:67
  86.2 53.6 %all-to-all-done.1.refs_3_ = bf16[4,640,256]{2,1,0:T(8,128)(2,1)S(1)} async-done(((bf16[4,640,256]{2,1,0:T(8,128)(2,1)}), bf16[4,640,256]{2,1,0:T(8,128)(2,1)S(1)}, u32[]{:S(2)}, u32[]{:S(2)}) %all-to-all-start.1) | async-done | bytes 1310752 | tf_op jit(solution)/shard_map/all_to_all | solution.py:276
  139.8 6.8 %all-to-all-start.2 = ((bf16[4,256,192]{1,2,0:T(8,128)(2,1)}), bf16[4,256,192]{1,2,0:T(8,128)(2,1)S(1)}, u32[]{:S(2)}, u32[]{:S(2)}) async-start(bf16[4,256,192]{1,2,0:T(8,128)(2,1)} %copy.17), calls=%async_computation.2 | async-start | bytes 786432 | tf_op jit(solution)/shard_map/all_to_all | solution.py:299
  147.4 13.8 %all-to-all-done.2 = bf16[4,256,192]{1,2,0:T(8,128)(2,1)S(1)} async-done(((bf16[4,256,192]{1,2,0:T(8,128)(2,1)}), bf16[4,256,192]{1,2,0:T(8,128)(2,1)S(1)}, u32[]{:S(2)}, u32[]{:S(2)}) %all-to-all-start.2) | async-done | bytes 393248 | tf_op jit(solution)/shard_map/all_to_all | solution.py:299
  162.0 3.5 %all-to-all-start.3 = ((bf16[4,256,192]{1,2,0:T(8,128)(2,1)}), bf16[4,256,192]{1,2,0:T(8,128)(2,1)S(1)}, u32[]{:S(2)}, u32[]{:S(2)}) async-start(bf16[4,256,192]{1,2,0:T(8,128)(2,1)} %broadcast_in_dim.54), calls=%async_computation.3 | async-start | bytes 786432 | tf_op jit(solution)/shard_map/all_to_all | solution.py:304
  165.5 9.7 %all-to-all-done.3 = bf16[4,256,192]{1,2,0:T(8,128)(2,1)S(1)} async-done(((bf16[4,256,192]{1,2,0:T(8,128)(2,1)}), bf16[4,256,192]{1,2,0:T(8,128)(2,1)S(1)}, u32[]{:S(2)}, u32[]{:S(2)}) %all-to-all-start.3) | async-done | bytes 393248 | tf_op jit(solution)/shard_map/all_to_all | solution.py:304
  175.4 4.5 %shard_map.129 = bf16[1024,1280]{1,0:T(8,128)(2,1)S(1)} custom-call(bf16[1024,192]{1,0:T(8,128)(2,1)S(1)} %bitcast.37, bf16[1024,2176]{1,0:T(8,128)(2,1)} %bitcast.1.x.marks, bf16[4,64,1024]{2,1,0:T(8,128)(2,1)S(1)} %copy-done.7, bf16[4,64,128]{2,1,0:T(8,128)(2,1)S(1)} %bitcast.40, bf16[4,64,128]{2,1,0:T(8,128)(2,1)S(1)} %bitcast.39), custom_call_target="tpu_custom_call" | custom-call | flops 671088640 | bytes 4194304 | tf_op jit(solution)/shard_map/pallas_call | solution.py:104
  179.9 1.5 copy-done.4
  181.4 6.6 %all-to-all-start.4 = ((bf16[32,32,1280]{2,1,0:T(8,128)(2,1)}), bf16[32,32,1280]{2,1,0:T(8,128)(2,1)S(1)}, u32[]{:S(2)}, u32[]{:S(2)}) async-start(bf16[32,32,1280]{2,1,0:T(8,128)(2,1)} %bitcast.35), calls=%async_computation.4 | async-start | bytes 5242880 | tf_op jit(solution)/shard_map/all_to_all | solution.py:308
  188.1 13.1 %convolution_bitcast_fusion.refs_2_ = f32[384,1024]{1,0:T(8,128)} fusion(bf16[4,384,2048]{2,1,0:T(8,128)(2,1)} %bitcast.45, bf16[4,2048,1024]{2,1,0:T(8,128)(2,1)} %bitcast.41), kind=kOutput, calls=%fused_computation | convolution fusion | flops 6442450944 | bytes 24641536 | tf_op jit(solution)/shard_map/tnf,tfc->nc/dot_general | solution.py:291
  201.2 19.1 %all-to-all-done.4.refs_4_ = bf16[32,32,1280]{2,1,0:T(8,128)(2,1)S(1)} async-done(((bf16[32,32,1280]{2,1,0:T(8,128)(2,1)}), bf16[32,32,1280]{2,1,0:T(8,128)(2,1)S(1)}, u32[]{:S(2)}, u32[]{:S(2)}) %all-to-all-start.4) | async-done | bytes 2621472 | tf_op jit(solution)/shard_map/all_to_all | solution.py:308
  220.3 1.3 copy-done.2
  221.6 1.4 copy-done.6
  223.0 10.0 %shard_map.130.refs_7_ = bf16[512,1024]{1,0:T(8,128)(2,1)} custom-call(s32[16]{0:T(128)S(1)} %multiply_add_fusion.refs_0_, s32[16]{0:T(128)S(1)} %copy-done.10, f32[384,1024]{1,0:T(8,128)S(1)} %copy-done.6, bf16[4,640,256]{2,1,0:T(8,128)(2,1)S(1)} %copy-done.2, bf16[32,32,1280]{2,1,0:T(8,128)(2,1)S(1)} %all-to-all-done.4.refs_4_, f32[128,128]{1,0:T(8,128)S(1)} %copy-done.8, ...), custom_call_target="tpu_custom_call" | custom-call | flops 201326592 | bytes 2359296 | tf_op jit(solution)/shard_map/pallas_call | solution.py:186
  233.0 8.8 %convolution_bitcast_fusion.1.refs_2_ = f32[128,1024]{1,0:T(8,128)S(1)} fusion(bf16[4,128,2048]{2,1,0:T(8,128)(2,1)} %bitcast.43, bf16[4,2048,1024]{2,1,0:T(8,128)(2,1)} %bitcast.42), kind=kOutput, calls=%fused_computation.3 | convolution fusion | flops 2147483648 | bytes 19398656 | tf_op jit(solution)/shard_map/tnf,tfc->nc/dot_general | solution.py:291
  241.8 4.1 %shard_map.131 = bf16[512,1024]{1,0:T(8,128)(2,1)} custom-call(s32[16]{0:T(128)S(1)} %multiply_add_fusion.refs_0_, s32[16]{0:T(128)S(1)} %copy-done.10, f32[128,1024]{1,0:T(8,128)S(1)} %convolution_bitcast_fusion.1.refs_2_, bf16[4,640,256]{2,1,0:T(8,128)(2,1)S(1)} %copy-done.3, ...), custom_call_target="tpu_custom_call", output_to_operand_aliasing={{}: (7, {})} | custom-call | flops 67108864 | bytes 786432 | tf_op jit(solution)/shard_map/pallas_call | solution.py:186
  (50 shorter events, 5.5 us)
Async XLA Ops:
  6.5 3.4 %copy-start.5 = (bf16[512,2048]{1,0:T(8,128)(2,1)S(1)}, bf16[512,2048]{1,0:T(8,128)(2,1)}, u32[]{:S(2)}) copy-start(bf16[512,2048]{1,0:T(8,128)(2,1)} %param.13) | copy-start | bytes 6291460
  6.5 2.9 %copy-start.14 = (s32[16]{0:T(128)S(1)}, s32[16]{0:T(128)}, u32[]{:S(2)}) copy-start(s32[16]{0:T(128)} %param.19) | copy-start | bytes 196
  6.5 2.9 %copy-start.13 = (s32[32]{0:T(128)S(1)}, s32[32]{0:T(128)}, u32[]{:S(2)}) copy-start(s32[32]{0:T(128)} %param.21) | copy-start | bytes 388
  6.5 181.5 %all-gather.7.cloned.1.call-start = ((), (), s32[]{:S(2)}) async-start(), calls=%async_computation.6 | async-start | bytes 7864320 | tf_op jit(solution)/shard_map/all_gather | solution.py:293
  10.9 2.1 copy-start
  13.1 5.3 %copy-start.12 = (bf16[4,64,256]{2,1,0:T(8,128)(2,1)S(1)}, bf16[4,64,256]{2,1,0:T(8,128)(2,1)}, u32[]{:S(2)}) copy-start(bf16[4,64,256]{2,1,0:T(8,128)(2,1)} %param.18) | copy-start | bytes 393220
  13.1 57.3 %all-to-all-start = ((bf16[32,32,2176]{2,1,0:T(8,128)(2,1)}), bf16[32,32,2176]{2,1,0:T(8,128)(2,1)}, u32[]{:S(2)}, u32[]{:S(2)}) async-start(bf16[32,32,2176]{2,1,0:T(8,128)(2,1)} %copy-done), calls=%async_computation | async-start | bytes 8912896 | tf_op jit(solution)/shard_map/all_to_all | solution.py:252
  70.4 69.4 %all-to-all-start.1 = ((bf16[4,640,256]{2,1,0:T(8,128)(2,1)}), bf16[4,640,256]{2,1,0:T(8,128)(2,1)S(1)}, u32[]{:S(2)}, u32[]{:S(2)}) async-start(bf16[4,640,256]{2,1,0:T(8,128)(2,1)} %pad_maximum_fusion), calls=%async_computation.1 | async-start | bytes 2621440 | tf_op jit(solution)/shard_map/all_to_all | solution.py:276
  76.9 1.9 copy-start.11
  139.8 35.6 %copy-start.1 = (bf16[4,640,256]{2,1,0:T(8,128)(2,1)}, bf16[4,640,256]{2,1,0:T(8,128)(2,1)S(1)}, u32[]{:S(2)}) copy-start(bf16[4,640,256]{2,1,0:T(8,128)(2,1)S(1)} %all-to-all-done.1.refs_3_) | copy-start | bytes 3932164
  139.8 21.4 %all-to-all-start.2 = ((bf16[4,256,192]{1,2,0:T(8,128)(2,1)}), bf16[4,256,192]{1,2,0:T(8,128)(2,1)S(1)}, u32[]{:S(2)}, u32[]{:S(2)}) async-start(bf16[4,256,192]{1,2,0:T(8,128)(2,1)} %copy.17), calls=%async_computation.2 | async-start | bytes 786432 | tf_op jit(solution)/shard_map/all_to_all | solution.py:299
  146.6 28.8 %copy-start.7 = (bf16[4,64,1024]{2,1,0:T(8,128)(2,1)S(1)}, bf16[4,64,1024]{2,1,0:T(8,128)(2,1)}, u32[]{:S(2)}) copy-start(bf16[4,64,1024]{2,1,0:T(8,128)(2,1)} %wq.1) | copy-start | bytes 1572868
  146.6 86.4 %all-gather.5.cloned.1.call-start = ((), (), s32[]{:S(2)}) async-start(), calls=%async_computation.5 | async-start | bytes 2621440 | tf_op jit(solution)/shard_map/all_gather | solution.py:295
  162.0 13.2 %all-to-all-start.3 = ((bf16[4,256,192]{1,2,0:T(8,128)(2,1)}), bf16[4,256,192]{1,2,0:T(8,128)(2,1)S(1)}, u32[]{:S(2)}, u32[]{:S(2)}) async-start(bf16[4,256,192]{1,2,0:T(8,128)(2,1)} %broadcast_in_dim.54), calls=%async_computation.3 | async-start | bytes 786432 | tf_op jit(solution)/shard_map/all_to_all | solution.py:304
  179.9 1.5 copy-start.4
  181.4 38.9 %all-to-all-start.4 = ((bf16[32,32,1280]{2,1,0:T(8,128)(2,1)}), bf16[32,32,1280]{2,1,0:T(8,128)(2,1)S(1)}, u32[]{:S(2)}, u32[]{:S(2)}) async-start(bf16[32,32,1280]{2,1,0:T(8,128)(2,1)} %bitcast.35), calls=%async_computation.4 | async-start | bytes 5242880 | tf_op jit(solution)/shard_map/all_to_all | solution.py:308
  188.1 32.2 %copy-start.8 = (f32[128,128]{1,0:T(8,128)S(1)}, f32[128,128]{1,0:T(8,128)}, u32[]{:S(2)}) copy-start(f32[128,128]{1,0:T(8,128)} %constant.77.clone.refs_5_) | copy-start | bytes 196612
  188.1 32.2 %copy-start.9 = (f32[128,128]{1,0:T(8,128)S(1)}, f32[128,128]{1,0:T(8,128)}, u32[]{:S(2)}) copy-start(f32[128,128]{1,0:T(8,128)} %constant.78.clone.refs_6_) | copy-start | bytes 196612
  188.1 32.2 %copy-start.10 = (s32[16]{0:T(128)S(1)}, s32[16]{0:T(128)}, u32[]{:S(2)}) copy-start(s32[16]{0:T(128)} %refs_1_.3) | copy-start | bytes 196
  220.3 1.3 copy-start.2
  221.6 1.4 copy-start.6
  233.0 8.8 %copy-start.3 = (bf16[4,640,256]{2,1,0:T(8,128)(2,1)S(1)}, bf16[4,640,256]{2,1,0:T(8,128)(2,1)}, u32[]{:S(2)}) copy-start(bf16[4,640,256]{2,1,0:T(8,128)(2,1)} %copy-done.1) | copy-start | bytes 3932164
Sparse Core Ops, SparseCore 0:
  9.6 154.3 all-gather.6
  165.5 44.0 all-gather.4

commit v4 on v3

--- a/solution.py
+++ b/solution.py
@@ -140,9 +140,7 @@
     def rotate(v):
         return (v * cos + pltpu.roll(v, HALF, 1) * sin).astype(jnp.bfloat16)
 
-    sums = pair[0].astype(jnp.float32)
-    for t in range(1, pair.shape[0]):
-        sums += pair[t].astype(jnp.float32)
+    sums = pair[...]
     keys_raw = (sums[:, :HEAD_SIZE] + change(query_cols, HEAD_SIZE)).astype(jnp.bfloat16)
     values = (sums[:, HEAD_SIZE:] + change(query_cols + HEAD_SIZE, HEAD_SIZE)).astype(jnp.bfloat16)
     keys = rotate(keys_raw.astype(jnp.float32))
@@ -191,9 +189,7 @@
             grid=(base_rows // rows,),
             in_specs=[
                 pl.BlockSpec((rows, query_cols), lambda i, *_: (i, 0)),
-                pl.BlockSpec(
-                    (pair.shape[0], rows, 2 * HEAD_SIZE), lambda i, *_: (0, first + i, 0)
-                ),
+                pl.BlockSpec((rows, 2 * HEAD_SIZE), lambda i, *_: (first + i, 0)),
                 whole(delta.shape),
                 whole(cosine.shape),
                 whole(sine.shape),
@@ -273,11 +269,23 @@
                 axis=1,
             )
         )
-    swapped = lax.all_to_all(jnp.stack(pieces), "tp", split_axis=0, concat_axis=0, tiled=True)
+    pieces = jnp.stack(pieces)
+    arrived = []
+    for step in range(tp_count):
+        piece = lax.dynamic_index_in_dim(pieces, (tp_here + step) % tp_count, 0, keepdims=False)
+        if step:
+            ring = [(t, (t + step) % tp_count) for t in range(tp_count)]
+            piece = lax.ppermute(piece, "tp", ring)
+        arrived.append(piece)
+    pair_here = arrived[0][:tok_rows].astype(jnp.float32)
+    for piece in arrived[1:]:
+        pair_here = pair_here + piece[:tok_rows].astype(jnp.float32)
+    ups = jnp.stack([piece[tok_rows:] for piece in arrived])
     head = tp_here // sharing
 
     def up_of(column):
-        both = lax.dynamic_index_in_dim(swapped, column // portion, 0, keepdims=False)[tok_rows:]
+        step = (tp_here - column // portion + tp_count) % tp_count
+        both = lax.dynamic_index_in_dim(ups, step, 0, keepdims=False)
         both = jnp.concatenate([both[:, :HEAD_SIZE], both[:, HEAD_SIZE:]], axis=0)
         return both.reshape(local_rows, rank, HEAD_SIZE)
 
@@ -312,7 +320,7 @@
         concat_axis=0,
         tiled=True,
     )
-    fixed = (swapped, returned, seq_len)
+    fixed = (pair_here, returned, seq_len)
     out = attend(slot_ids, request_token_length, project(first), *fixed, 0, tok_rows, None)
     second, out = lax.optimization_barrier((second, out))
     return attend(slot_ids, request_token_length, project(second), *fixed, early, tok_rows, out)

time: 254 us -> 238 us (0.937)
  waiting for transfers between devices: 142 us -> 128 us
  starting transfers between devices: 27.9 us -> 23.8 us
    all_to_all x1 -> x0, waiting for transfers between devices: 53.6 us -> none  [shards(): lax.all_to_all(jnp.stack(pieces), 'tp', split_axis=0, concat_axis=0, tile...]
    ppermute x0 -> x3, waiting for transfers between devices: none -> 32.8 us  [shards(): piece = lax.ppermute(piece, 'tp', ring)]
    all_to_all x1, waiting for transfers between devices: 45.3 us -> 17.4 us  [shards(): lax.all_to_all(send, 'rep', split_axis=0, concat_axis=0, tiled=True)]
    all_gather x1, waiting for transfers between devices: 0.01 us -> 21.3 us  [shards(): second = lax.all_gather(late_rows, 'tp', axis=0, tiled=False)]
    all_to_all x1, waiting for transfers between devices: 19.1 us -> 0.01 us  [shards(): lax.all_to_all(delta.reshape(slot_count, seq_len, delta.shape[1]), 'rep',...]
    all_gather x1, waiting for transfers between devices: 0.01 us -> 18.5 us  [shards(): first = lax.all_gather(tokens[:early], 'tp', axis=0, tiled=False)]
    all_to_all x1, waiting for transfers between devices: 9.67 us -> 20.9 us  [shards(): shrink = lax.all_to_all(own, 'tp', split_axis=0, concat_axis=0, tiled=True)]
    all_to_all x1 -> x0, starting transfers between devices: 5.65 us -> none  [shards(): lax.all_to_all(jnp.stack(pieces), 'tp', split_axis=0, concat_axis=0, tile...]
  transfers between devices with their start and end apart: 7 -> 9, of which waited for: 5 -> 7; matrix products, arithmetic and copies ran while one was open for 9% -> 12% of each run, Pallas kernels for 9% -> 9%
where the time goes in v4:
time: 238 us
  waiting for transfers between devices  128 us (54%)
  matrix products  26.8 us (11%)
  Pallas kernels  25.8 us (11%)
  starting transfers between devices  23.8 us (10%)
  local copies, waits for them, and re-layouts  15.9 us (7%)
  between operations  13.7 us (6%)
  other arithmetic  3.29 us (1%)
    ppermute x3, waiting for transfers between devices, shards(): piece = lax.ppermute(piece, 'tp', ring)  32.8 us
    dot_general x2, matrix products, project(): jnp.einsum('tnf,tfc->nc', gathered, weight, preferred_element_type=jnp.fl...  21.8 us
    all_gather x1, waiting for transfers between devices, shards(): second = lax.all_gather(late_rows, 'tp', axis=0, tiled=False)  21.3 us
    all_to_all x1, waiting for transfers between devices, shards(): shrink = lax.all_to_all(own, 'tp', split_axis=0, concat_axis=0, tiled=True)  20.9 us
    all_gather x1, waiting for transfers between devices, shards(): first = lax.all_gather(tokens[:early], 'tp', axis=0, tiled=False)  18.5 us
    all_to_all x1, waiting for transfers between devices, shards(): lax.all_to_all(partial, 'tp', split_axis=0, concat_axis=0, tiled=True)  17.4 us
    all_to_all x1, waiting for transfers between devices, shards(): lax.all_to_all(send, 'rep', split_axis=0, concat_axis=0, tiled=True)  17.4 us
    pallas_call x2, Pallas kernels, attend(): pl.pallas_call(body, out_shape=jax.ShapeDtypeStruct((tok_rows, query_cols...  14 us
  transfers between devices with their start and end apart: 9, of which 7 were waited for; matrix products, arithmetic and copies ran while one was open for 12% of the time, Pallas kernels for 9%

profile of v4, /device:TPU:0, one launch (start us, length us, event | category | flops | bytes accessed | tf_op | source)
XLA Modules:
  0.0 237.6 jit_solution(4335433543275260406)
XLA Ops:
  6.5 2.9 %slice.105 = bf16[384,2048]{1,0:T(8,128)(2,1)} slice(bf16[512,2048]{1,0:T(8,128)(2,1)} %param.13), slice={[0:384], [0:2048]} | slice | bytes 3145728 | tf_op jit(solution)/shard_map/slice | solution.py:301
  11.0 2.1 copy-done
  13.1 5.3 %all-to-all-start = ((bf16[32,32,2176]{2,1,0:T(8,128)(2,1)}), bf16[32,32,2176]{2,1,0:T(8,128)(2,1)}, u32[]{:S(2)}, u32[]{:S(2)}) async-start(bf16[32,32,2176]{2,1,0:T(8,128)(2,1)} %copy-done), calls=%async_computation | async-start | bytes 8912896 | tf_op jit(solution)/shard_map/all_to_all | solution.py:248
  18.4 5.0 %convolution_convert_fusion = bf16[512,1024]{1,0:T(8,128)(2,1)S(1)} fusion(bf16[512,2048]{1,0:T(8,128)(2,1)S(1)} %copy-done.2, bf16[2048,1024]{1,0:T(8,128)(2,1)} %param.15), kind=kOutput, calls=%fused_computation.1 | convolution fusion | flops 2148007936 | bytes 7340032 | tf_op jit(solution)/shard_map/dot_general | solution.py:251
  25.0 2.1 dynamic-slice_bitcast_fusion.2
  27.2 4.6 %collective-permute-start.2 = (bf16[640,256]{1,0:T(8,128)(2,1)}, bf16[640,256]{1,0:T(8,128)(2,1)S(1)}, u32[]{:S(2)}, u32[]{:S(2)}) collective-permute-start(bf16[640,256]{1,0:T(8,128)(2,1)} %get-tuple-element.16), channel_id=1, source_target_pairs={{0,3},{1,0},{2,1},{3,2},{4,7},{5,4},{6,5},{7,6},{8,11},{9,8},{10,9... | collective-permute-start | bytes 983048 | tf_op jit(solution)/shard_map/ppermute | solution.py:278
  34.4 18.6 %collective-permute-done.2 = bf16[640,256]{1,0:T(8,128)(2,1)S(1)} collective-permute-done((bf16[640,256]{1,0:T(8,128)(2,1)}, bf16[640,256]{1,0:T(8,128)(2,1)S(1)}, u32[]{:S(2)}, u32[]{:S(2)}) %collective-permute-start.2) | collective-permute-done | bytes 327712 | tf_op jit(solution)/shard_map/ppermute | solution.py:278
  53.0 17.4 %all-to-all-done = bf16[32,32,2176]{2,1,0:T(8,128)(2,1)} async-done(((bf16[32,32,2176]{2,1,0:T(8,128)(2,1)}), bf16[32,32,2176]{2,1,0:T(8,128)(2,1)}, u32[]{:S(2)}, u32[]{:S(2)}) %all-to-all-start) | async-done | bytes 4456480 | tf_op jit(solution)/shard_map/all_to_all | solution.py:248
  70.4 1.9 copy-done.8
  72.3 6.4 %shard_map.128 = bf16[1024,192]{1,0:T(8,128)(2,1)S(1)} custom-call(bf16[1024,2176]{1,0:T(8,128)(2,1)} %bitcast.1.x.marks, bf16[4,192,2048]{2,1,0:T(8,128)(2,1)S(1)} %copy-done.8), custom_call_target="tpu_custom_call" | custom-call | flops 3221225472 | bytes 9437184 | tf_op jit(solution)/shard_map/pallas_call | solution.py:67
  79.6 5.6 %all-to-all-start.1 = ((bf16[4,256,192]{1,2,0:T(8,128)(2,1)}), bf16[4,256,192]{1,2,0:T(8,128)(2,1)S(1)}, u32[]{:S(2)}, u32[]{:S(2)}) async-start(bf16[4,256,192]{1,2,0:T(8,128)(2,1)} %copy.17), calls=%async_computation.1 | async-start | bytes 786432 | tf_op jit(solution)/shard_map/all_to_all | solution.py:307
  85.3 14.2 %collective-permute-done.1 = bf16[640,256]{1,0:T(8,128)(2,1)S(1)} collective-permute-done((bf16[640,256]{1,0:T(8,128)(2,1)}, bf16[640,256]{1,0:T(8,128)(2,1)S(1)}, u32[]{:S(2)}, u32[]{:S(2)}) %collective-permute-start.1) | collective-permute-done | bytes 327712 | tf_op jit(solution)/shard_map/ppermute | solution.py:278
  99.7 17.4 %all-to-all-done.1 = bf16[4,256,192]{1,2,0:T(8,128)(2,1)S(1)} async-done(((bf16[4,256,192]{1,2,0:T(8,128)(2,1)}), bf16[4,256,192]{1,2,0:T(8,128)(2,1)S(1)}, u32[]{:S(2)}, u32[]{:S(2)}) %all-to-all-start.1) | async-done | bytes 393248 | tf_op jit(solution)/shard_map/all_to_all | solution.py:307
  117.9 3.5 %all-to-all-start.2 = ((bf16[4,256,192]{1,2,0:T(8,128)(2,1)}), bf16[4,256,192]{1,2,0:T(8,128)(2,1)S(1)}, u32[]{:S(2)}, u32[]{:S(2)}) async-start(bf16[4,256,192]{1,2,0:T(8,128)(2,1)} %broadcast_in_dim.54), calls=%async_computation.2 | async-start | bytes 786432 | tf_op jit(solution)/shard_map/all_to_all | solution.py:312
  121.4 20.9 %all-to-all-done.2 = bf16[4,256,192]{1,2,0:T(8,128)(2,1)S(1)} async-done(((bf16[4,256,192]{1,2,0:T(8,128)(2,1)}), bf16[4,256,192]{1,2,0:T(8,128)(2,1)S(1)}, u32[]{:S(2)}, u32[]{:S(2)}) %all-to-all-start.2) | async-done | bytes 393248 | tf_op jit(solution)/shard_map/all_to_all | solution.py:312
  142.6 4.5 %shard_map.129 = bf16[1024,1280]{1,0:T(8,128)(2,1)S(1)} custom-call(bf16[1024,192]{1,0:T(8,128)(2,1)S(1)} %bitcast.54, bf16[1024,2176]{1,0:T(8,128)(2,1)} %bitcast.1.x.marks, bf16[4,64,1024]{2,1,0:T(8,128)(2,1)S(1)} %copy-done.4, bf16[4,64,128]{2,1,0:T(8,128)(2,1)S(1)} %bitcast.57, bf16[4,64,128]{2,1,0:T(8,128)(2,1)S(1)} %bitcast.56), custom_call_target="tpu_custom_call" | custom-call | flops 671088640 | bytes 4194304 | tf_op jit(solution)/shard_map/pallas_call | solution.py:104
  147.1 1.5 copy-done.1
  148.6 3.8 %all-to-all-start.3 = ((bf16[32,32,1280]{2,1,0:T(8,128)(2,1)}), bf16[32,32,1280]{2,1,0:T(8,128)(2,1)S(1)}, u32[]{:S(2)}, u32[]{:S(2)}) async-start(bf16[32,32,1280]{2,1,0:T(8,128)(2,1)} %bitcast.52), calls=%async_computation.3 | async-start | bytes 5242880 | tf_op jit(solution)/shard_map/all_to_all | solution.py:316
  153.8 18.5 %all-gather.7.cloned.1.call-done = bf16[1536,2048]{1,0:T(8,128)(2,1)} async-done(((bf16[384,2048]{1,0:T(8,128)(2,1)}), bf16[1536,2048]{1,0:T(8,128)(2,1)}) %all-gather.7.cloned.1.call-update) | async-done | bytes 6291472 | tf_op jit(solution)/shard_map/all_gather | solution.py:301
  172.2 13.0 %convolution_bitcast_fusion.refs_2_ = f32[384,1024]{1,0:T(8,128)} fusion(bf16[4,384,2048]{2,1,0:T(8,128)(2,1)} %bitcast.62, bf16[4,2048,1024]{2,1,0:T(8,128)(2,1)} %bitcast.58), kind=kOutput, calls=%fused_computation | convolution fusion | flops 6442450944 | bytes 24641536 | tf_op jit(solution)/shard_map/tnf,tfc->nc/dot_general | solution.py:299
  186.7 9.8 %shard_map.130.refs_7_ = bf16[512,1024]{1,0:T(8,128)(2,1)} custom-call(s32[16]{0:T(128)S(1)} %multiply_add_fusion.refs_0_, s32[16]{0:T(128)S(1)} %copy-done.7, f32[384,1024]{1,0:T(8,128)S(1)} %copy-done.3, f32[512,256]{1,0:T(8,128)S(1)} %fusion.1.refs_3_, bf16[32,32,1280]{2,1,0:T(8,128)(2,1)S(1)} %all-to-all-done.3.refs_4_, f32[128,128]{1,0:T(8,128)S(1)} %copy-done.5, ...), custom_call_target="tpu_custom_call" | custom-call | flops 201326592 | bytes 2359296 | tf_op jit(solution)/shard_map/pallas_call | solution.py:184
  196.6 21.3 %all-gather.5.cloned.1.call-done = bf16[512,2048]{1,0:T(8,128)(2,1)} async-done(((bf16[128,2048]{1,0:T(8,128)(2,1)}), bf16[512,2048]{1,0:T(8,128)(2,1)}) %all-gather.5.cloned.1.call-update) | async-done | bytes 2097168 | tf_op jit(solution)/shard_map/all_gather | solution.py:303
  217.9 8.7 %convolution_bitcast_fusion.1.refs_2_ = f32[128,1024]{1,0:T(8,128)S(1)} fusion(bf16[4,128,2048]{2,1,0:T(8,128)(2,1)} %bitcast.60, bf16[4,2048,1024]{2,1,0:T(8,128)(2,1)} %bitcast.59), kind=kOutput, calls=%fused_computation.3 | convolution fusion | flops 2147483648 | bytes 19398656 | tf_op jit(solution)/shard_map/tnf,tfc->nc/dot_general | solution.py:299
  226.6 4.1 %shard_map.131 = bf16[512,1024]{1,0:T(8,128)(2,1)} custom-call(s32[16]{0:T(128)S(1)} %multiply_add_fusion.refs_0_, s32[16]{0:T(128)S(1)} %copy-done.7, f32[128,1024]{1,0:T(8,128)S(1)} %convolution_bitcast_fusion.1.refs_2_, f32[512,256]{1,0:T(8,128)S(1)} %fusion.1.refs_3_, ...), custom_call_target="tpu_custom_call", output_to_operand_aliasing={{}: (7, {})} | custom-call | flops 67108864 | bytes 786432 | tf_op jit(solution)/shard_map/pallas_call | solution.py:184
  (61 shorter events, 10.7 us)
Async XLA Ops:
  6.5 3.4 %copy-start.2 = (bf16[512,2048]{1,0:T(8,128)(2,1)S(1)}, bf16[512,2048]{1,0:T(8,128)(2,1)}, u32[]{:S(2)}) copy-start(bf16[512,2048]{1,0:T(8,128)(2,1)} %param.13) | copy-start | bytes 6291460
  6.5 2.9 %copy-start.14 = (s32[16]{0:T(128)S(1)}, s32[16]{0:T(128)}, u32[]{:S(2)}) copy-start(s32[16]{0:T(128)} %param.19) | copy-start | bytes 196
  6.5 2.9 %copy-start.13 = (s32[32]{0:T(128)S(1)}, s32[32]{0:T(128)}, u32[]{:S(2)}) copy-start(s32[32]{0:T(128)} %param.21) | copy-start | bytes 388
  6.5 165.7 %all-gather.7.cloned.1.call-start = ((), (), s32[]{:S(2)}) async-start(), calls=%async_computation.5 | async-start | bytes 7864320 | tf_op jit(solution)/shard_map/all_gather | solution.py:301
  10.9 2.1 copy-start
  13.1 5.3 %copy-start.12 = (bf16[4,64,256]{2,1,0:T(8,128)(2,1)S(1)}, bf16[4,64,256]{2,1,0:T(8,128)(2,1)}, u32[]{:S(2)}) copy-start(bf16[4,64,256]{2,1,0:T(8,128)(2,1)} %param.18) | copy-start | bytes 393220
  13.1 57.3 %all-to-all-start = ((bf16[32,32,2176]{2,1,0:T(8,128)(2,1)}), bf16[32,32,2176]{2,1,0:T(8,128)(2,1)}, u32[]{:S(2)}, u32[]{:S(2)}) async-start(bf16[32,32,2176]{2,1,0:T(8,128)(2,1)} %copy-done), calls=%async_computation | async-start | bytes 8912896 | tf_op jit(solution)/shard_map/all_to_all | solution.py:248
  27.2 25.8 %collective-permute-start.2 = (bf16[640,256]{1,0:T(8,128)(2,1)}, bf16[640,256]{1,0:T(8,128)(2,1)S(1)}, u32[]{:S(2)}, u32[]{:S(2)}) collective-permute-start(bf16[640,256]{1,0:T(8,128)(2,1)} %get-tuple-element.16), channel_id=1, source_target_pairs={{0,3},{1,0},{2,1},{3,2},{4,7},{5,4},{6,5},{7,6},{8,11},{9,8},{10,9... | collective-permute-start | bytes 983048 | tf_op jit(solution)/shard_map/ppermute | solution.py:278
  31.7 67.8 %collective-permute-start.1 = (bf16[640,256]{1,0:T(8,128)(2,1)}, bf16[640,256]{1,0:T(8,128)(2,1)S(1)}, u32[]{:S(2)}, u32[]{:S(2)}) collective-permute-start(bf16[640,256]{1,0:T(8,128)(2,1)} %get-tuple-element.17), channel_id=1, source_target_pairs={{0,2},{1,3},{2,0},{3,1},{4,6},{5,7},{6,4},{7,5},{8,10},{9,11},{10,... | collective-permute-start | bytes 983048 | tf_op jit(solution)/shard_map/ppermute | solution.py:278
  31.7 67.8 %collective-permute-start = (bf16[640,256]{1,0:T(8,128)(2,1)}, bf16[640,256]{1,0:T(8,128)(2,1)S(1)}, u32[]{:S(2)}, u32[]{:S(2)}) collective-permute-start(bf16[640,256]{1,0:T(8,128)(2,1)} %get-tuple-element.15), channel_id=1, source_target_pairs={{0,1},{1,2},{2,3},{3,0},{4,5},{5,6},{6,7},{7,4},{8,9},{9,10},{10,1... | collective-permute-start | bytes 983048 | tf_op jit(solution)/shard_map/ppermute | solution.py:278
  53.0 25.7 %copy-start.9 = (bf16[640,256]{1,0:T(8,128)(2,1)}, bf16[640,256]{1,0:T(8,128)(2,1)S(1)}, u32[]{:S(2)}) copy-start(bf16[640,256]{1,0:T(8,128)(2,1)S(1)} %collective-permute-done.2) | copy-start | bytes 983044
  70.4 1.9 copy-start.8
  79.6 37.4 %all-to-all-start.1 = ((bf16[4,256,192]{1,2,0:T(8,128)(2,1)}), bf16[4,256,192]{1,2,0:T(8,128)(2,1)S(1)}, u32[]{:S(2)}, u32[]{:S(2)}) async-start(bf16[4,256,192]{1,2,0:T(8,128)(2,1)} %copy.17), calls=%async_computation.1 | async-start | bytes 786432 | tf_op jit(solution)/shard_map/all_to_all | solution.py:307
  85.3 132.6 %all-gather.5.cloned.1.call-start = ((), (), s32[]{:S(2)}) async-start(), calls=%async_computation.4 | async-start | bytes 2621440 | tf_op jit(solution)/shard_map/all_gather | solution.py:303
  99.5 43.1 %copy-start.10 = (bf16[640,256]{1,0:T(8,128)(2,1)}, bf16[640,256]{1,0:T(8,128)(2,1)S(1)}, u32[]{:S(2)}) copy-start(bf16[640,256]{1,0:T(8,128)(2,1)S(1)} %collective-permute-done.1) | copy-start | bytes 983044
  99.5 43.0 %copy-start.11 = (bf16[640,256]{1,0:T(8,128)(2,1)}, bf16[640,256]{1,0:T(8,128)(2,1)S(1)}, u32[]{:S(2)}) copy-start(bf16[640,256]{1,0:T(8,128)(2,1)S(1)} %collective-permute-done) | copy-start | bytes 983044
  99.6 43.0 %copy-start.4 = (bf16[4,64,1024]{2,1,0:T(8,128)(2,1)S(1)}, bf16[4,64,1024]{2,1,0:T(8,128)(2,1)}, u32[]{:S(2)}) copy-start(bf16[4,64,1024]{2,1,0:T(8,128)(2,1)} %wq.1) | copy-start | bytes 1572868
  117.9 24.5 %all-to-all-start.2 = ((bf16[4,256,192]{1,2,0:T(8,128)(2,1)}), bf16[4,256,192]{1,2,0:T(8,128)(2,1)S(1)}, u32[]{:S(2)}, u32[]{:S(2)}) async-start(bf16[4,256,192]{1,2,0:T(8,128)(2,1)} %broadcast_in_dim.54), calls=%async_computation.2 | async-start | bytes 786432 | tf_op jit(solution)/shard_map/all_to_all | solution.py:312
  147.1 1.5 copy-start.1
  148.6 36.7 %all-to-all-start.3 = ((bf16[32,32,1280]{2,1,0:T(8,128)(2,1)}), bf16[32,32,1280]{2,1,0:T(8,128)(2,1)S(1)}, u32[]{:S(2)}, u32[]{:S(2)}) async-start(bf16[32,32,1280]{2,1,0:T(8,128)(2,1)} %bitcast.52), calls=%async_computation.3 | async-start | bytes 5242880 | tf_op jit(solution)/shard_map/all_to_all | solution.py:316
  172.2 13.1 %copy-start.5 = (f32[128,128]{1,0:T(8,128)S(1)}, f32[128,128]{1,0:T(8,128)}, u32[]{:S(2)}) copy-start(f32[128,128]{1,0:T(8,128)} %constant.115.clone.refs_5_) | copy-start | bytes 196612
  172.2 13.1 %copy-start.6 = (f32[128,128]{1,0:T(8,128)S(1)}, f32[128,128]{1,0:T(8,128)}, u32[]{:S(2)}) copy-start(f32[128,128]{1,0:T(8,128)} %constant.116.clone.refs_6_) | copy-start | bytes 196612
  172.2 13.1 %copy-start.7 = (s32[16]{0:T(128)S(1)}, s32[16]{0:T(128)}, u32[]{:S(2)}) copy-start(s32[16]{0:T(128)} %refs_1_.3) | copy-start | bytes 196
  185.3 1.4 copy-start.3
Sparse Core Ops, SparseCore 0:
  9.6 162.6 all-gather.6
  173.8 44.0 all-gather.4

commit v5 on v4

--- a/solution.py
+++ b/solution.py
@@ -298,9 +298,20 @@
     def project(gathered):
         return jnp.einsum("tnf,tfc->nc", gathered, weight, preferred_element_type=jnp.float32)
 
-    first = lax.all_gather(tokens[:early], "tp", axis=0, tiled=False)
-    late_rows, received = lax.optimization_barrier((tokens[early:], received))
-    second = lax.all_gather(late_rows, "tp", axis=0, tiled=False)
+    rightward = [(t, t + 1) for t in range(tp_count - 1)]
+    leftward = [(t + 1, t) for t in range(tp_count - 1)]
+
+    def line_gather(block):
+        from_left, from_right = [block], [block]
+        for _ in range(tp_count - 1):
+            from_left.append(lax.ppermute(from_left[-1], "tp", rightward))
+            from_right.append(lax.ppermute(from_right[-1], "tp", leftward))
+        turned = [block] + [from_left[k] + from_right[tp_count - k] for k in range(1, tp_count)]
+        order = (tp_here - jnp.arange(tp_count) + tp_count) % tp_count
+        return jnp.take(jnp.stack(turned), order, axis=0, mode="clip")
+
+    first = line_gather(tokens[:early])
+    second = line_gather(tokens[early:])
 
     partial = down_project(received, adapter_down_tables)
     partial = partial.reshape(tp_count, slot_count * seq_len // tp_count, 3 * rank)

time: 238 us -> 284 us (1.19)
  starting transfers between devices: 23.8 us -> 73.8 us
  waiting for transfers between devices: 128 us -> 110 us
  other arithmetic: 3.29 us -> 20.2 us
  between operations: 13.7 us -> 0.43 us
  local copies, waits for them, and re-layouts: 15.9 us -> 26.2 us
    ppermute x0 -> x12, waiting for transfers between devices: none -> 42.8 us  [the longest x6 23 us: line_gather(): from_left.append(lax.ppermute(from_left[-1], 'tp', rightward))]
    all_gather x2 -> x0, waiting for transfers between devices: 39.7 us -> none  [the longest x1 21.3 us: shards(): second = lax.all_gather(late_rows, 'tp', axis=0, tiled=False)]
    ppermute x0 -> x12, starting transfers between devices: none -> 36.2 us  [the longest x6 28.5 us: line_gather(): from_left.append(lax.ppermute(from_left[-1], 'tp', rightward))]
    all_to_all x1, waiting for transfers between devices: 17.4 us -> 0.01 us  [shards(): lax.all_to_all(send, 'rep', split_axis=0, concat_axis=0, tiled=True)]
    another operation x0 -> x8, other arithmetic: none -> 17.1 us  [line_gather(): return jnp.take(jnp.stack(turned), order, axis=0, mode='clip')]
    ppermute x3, starting transfers between devices: 5.59 us -> 16.6 us  [shards(): piece = lax.ppermute(piece, 'tp', ring)]
    gather x0 -> x2, local copies, waits for them, and re-layouts: none -> 8.44 us  [line_gather(): return jnp.take(jnp.stack(turned), order, axis=0, mode='clip')]
    all_to_all x1, waiting for transfers between devices: 0.01 us -> 6.27 us  [shards(): lax.all_to_all(delta.reshape(slot_count, seq_len, delta.shape[1]), 'rep',...]
  transfers between devices with their start and end apart: 9 -> 19, of which waited for: 7 -> 9; matrix products, arithmetic and copies ran while one was open for 12% -> 19% of each run, Pallas kernels for 9% -> 4%
where the time goes in v5:
time: 284 us; the launch traced here: 283 us
  waiting for transfers between devices  110 us (39%)
  starting transfers between devices  73.8 us (26%)
  matrix products  26.9 us (9%)
  local copies, waits for them, and re-layouts  26.2 us (9%)
  Pallas kernels  25.8 us (9%)
  other arithmetic  20.2 us (7%)
    ppermute x3, waiting for transfers between devices, shards(): piece = lax.ppermute(piece, 'tp', ring)  30.4 us
    ppermute x6, starting transfers between devices, line_gather(): from_left.append(lax.ppermute(from_left[-1], 'tp', rightward))  28.5 us
    ppermute x6, waiting for transfers between devices, line_gather(): from_left.append(lax.ppermute(from_left[-1], 'tp', rightward))  23 us
    dot_general x2, matrix products, project(): jnp.einsum('tnf,tfc->nc', gathered, weight, preferred_element_type=jnp.fl...  21.3 us
    ppermute x6, waiting for transfers between devices, line_gather(): from_right.append(lax.ppermute(from_right[-1], 'tp', leftward))  19.8 us
    another operation x8, other arithmetic, line_gather(): return jnp.take(jnp.stack(turned), order, axis=0, mode='clip')  17.1 us
    ppermute x3, starting transfers between devices, shards(): piece = lax.ppermute(piece, 'tp', ring)  16.6 us
    all_to_all x1, waiting for transfers between devices, shards(): lax.all_to_all(partial, 'tp', split_axis=0, concat_axis=0, tiled=True)  15.3 us
  transfers between devices with their start and end apart: 19, of which 9 were waited for; matrix products, arithmetic and copies ran while one was open for 19% of the time, Pallas kernels for 4%

profile of v5, /device:TPU:0, one launch (start us, length us, event | category | flops | bytes accessed | tf_op | source)
XLA Modules:
  0.0 283.0 jit_solution(5423760678892237589)
XLA Ops:
  2.0 5.9 %collective-permute-start = (bf16[128,2048]{1,0:T(8,128)(2,1)}, bf16[128,2048]{1,0:T(8,128)(2,1)}, u32[]{:S(2)}, u32[]{:S(2)}) collective-permute-start(bf16[128,2048]{1,0:T(8,128)(2,1)} %get-tuple-element.14), channel_id=1, source_target_pairs={{0,1},{1,2},{2,3},{4,5},{5,6},{6,7},{8,9},{9,10},{10,11},{12,13},{... | collective-permute-start | bytes 1572872 | tf_op jit(solution)/shard_map/ppermute | solution.py:307
  12.8 5.7 %collective-permute-start.6 = (bf16[384,2048]{1,0:T(8,128)(2,1)}, bf16[384,2048]{1,0:T(8,128)(2,1)}, u32[]{:S(2)}, u32[]{:S(2)}) collective-permute-start(bf16[384,2048]{1,0:T(8,128)(2,1)} %get-tuple-element.12), channel_id=1, source_target_pairs={{0,1},{1,2},{2,3},{4,5},{5,6},{6,7},{8,9},{9,10},{10,11},{12,13},{... | collective-permute-start | bytes 4718600 | tf_op jit(solution)/shard_map/ppermute | solution.py:307
  22.0 4.6 %all-to-all-start = ((bf16[32,32,2176]{2,1,0:T(8,128)(2,1)}), bf16[32,32,2176]{2,1,0:T(8,128)(2,1)}, u32[]{:S(2)}, u32[]{:S(2)}) async-start(bf16[32,32,2176]{2,1,0:T(8,128)(2,1)} %copy-done), calls=%async_computation | async-start | bytes 8912896 | tf_op jit(solution)/shard_map/all_to_all | solution.py:248
  26.6 5.6 %convolution_convert_fusion = bf16[512,1024]{1,0:T(8,128)(2,1)} fusion(bf16[512,2048]{1,0:T(8,128)(2,1)S(1)} %copy-done.2, bf16[2048,1024]{1,0:T(8,128)(2,1)} %param.15), kind=kOutput, calls=%fused_computation.8 | convolution fusion | flops 2148007936 | bytes 7340032 | tf_op jit(solution)/shard_map/dot_general | solution.py:251
  38.7 21.7 %collective-permute-done.12 = bf16[640,256]{1,0:T(8,128)(2,1)S(1)} collective-permute-done((bf16[640,256]{1,0:T(8,128)(2,1)}, bf16[640,256]{1,0:T(8,128)(2,1)S(1)}, u32[]{:S(2)}, u32[]{:S(2)}) %collective-permute-start.12) | collective-permute-done | bytes 327712 | tf_op jit(solution)/shard_map/ppermute | solution.py:278
  60.4 12.8 %collective-permute-start.13 = (bf16[640,256]{1,0:T(8,128)(2,1)S(1)}, bf16[640,256]{1,0:T(8,128)(2,1)S(1)}, u32[]{:S(2)}, u32[]{:S(2)}) collective-permute-start(bf16[640,256]{1,0:T(8,128)(2,1)S(1)} %get-tuple-element.17), channel_id=1, source_target_pairs={{0,2},{1,3},{2,0},{3,1},{4,6},{5,7},{6,4},{7,5},{8,10},{9,11},{10,... | collective-permute-start | bytes 983048 | tf_op jit(solution)/shard_map/ppermute | solution.py:278
  74.5 8.8 %collective-permute-done.13 = bf16[640,256]{1,0:T(8,128)(2,1)S(1)} collective-permute-done((bf16[640,256]{1,0:T(8,128)(2,1)S(1)}, bf16[640,256]{1,0:T(8,128)(2,1)S(1)}, u32[]{:S(2)}, u32[]{:S(2)}) %collective-permute-start.13) | collective-permute-done | bytes 327712 | tf_op jit(solution)/shard_map/ppermute | solution.py:278
  86.0 5.7 %collective-permute-start.10 = (bf16[384,2048]{1,0:T(8,128)(2,1)}, bf16[384,2048]{1,0:T(8,128)(2,1)}, u32[]{:S(2)}, u32[]{:S(2)}) collective-permute-start(bf16[384,2048]{1,0:T(8,128)(2,1)} %collective-permute-done.6), channel_id=1, source_target_pairs={{0,1},{1,2},{2,3},{4,5},{5,6},{6,7},{8,9},{9,10},{10,11},{12,13},{... | collective-permute-start | bytes 4718600 | tf_op jit(solution)/shard_map/ppermute | solution.py:307
  92.8 4.5 %collective-permute-done.4 = bf16[128,2048]{1,0:T(8,128)(2,1)S(1)} collective-permute-done((bf16[128,2048]{1,0:T(8,128)(2,1)}, bf16[128,2048]{1,0:T(8,128)(2,1)S(1)}, u32[]{:S(2)}, u32[]{:S(2)}) %collective-permute-start.4) | collective-permute-done | bytes 524320 | tf_op jit(solution)/shard_map/ppermute | solution.py:307
  97.3 4.3 %collective-permute-start.5 = (bf16[128,2048]{1,0:T(8,128)(2,1)S(1)}, bf16[128,2048]{1,0:T(8,128)(2,1)S(1)}, u32[]{:S(2)}, u32[]{:S(2)}) collective-permute-start(bf16[128,2048]{1,0:T(8,128)(2,1)S(1)} %collective-permute-done.4), channel_id=1, source_target_pairs={{0,1},{1,2},{2,3},{4,5},{5,6},{6,7},{8,9},{9,10},{10,11},{12,13},{... | collective-permute-start | bytes 1572872 | tf_op jit(solution)/shard_map/ppermute | solution.py:307
  101.7 16.7 %collective-permute-done.2 = bf16[128,2048]{1,0:T(8,128)(2,1)S(1)} collective-permute-done((bf16[128,2048]{1,0:T(8,128)(2,1)}, bf16[128,2048]{1,0:T(8,128)(2,1)S(1)}, u32[]{:S(2)}, u32[]{:S(2)}) %collective-permute-start.2) | collective-permute-done | bytes 524320 | tf_op jit(solution)/shard_map/ppermute | solution.py:308
  121.9 18.5 %collective-permute-done.5 = bf16[128,2048]{1,0:T(8,128)(2,1)S(1)} collective-permute-done((bf16[128,2048]{1,0:T(8,128)(2,1)S(1)}, bf16[128,2048]{1,0:T(8,128)(2,1)S(1)}, u32[]{:S(2)}, u32[]{:S(2)}) %collective-permute-start.5) | collective-permute-done | bytes 524320 | tf_op jit(solution)/shard_map/ppermute | solution.py:307
  142.2 5.5 %collective-permute-start.11 = (bf16[384,2048]{1,0:T(8,128)(2,1)}, bf16[384,2048]{1,0:T(8,128)(2,1)}, u32[]{:S(2)}, u32[]{:S(2)}) collective-permute-start(bf16[384,2048]{1,0:T(8,128)(2,1)} %collective-permute-done.10), channel_id=1, source_target_pairs={{0,1},{1,2},{2,3},{4,5},{5,6},{6,7},{8,9},{9,10},{10,11},{12,13},{... | collective-permute-start | bytes 4718600 | tf_op jit(solution)/shard_map/ppermute | solution.py:307
  149.7 6.4 %shard_map.128 = bf16[1024,192]{1,0:T(8,128)(2,1)S(1)} custom-call(bf16[1024,2176]{1,0:T(8,128)(2,1)} %bitcast.21.x.marks, bf16[4,192,2048]{2,1,0:T(8,128)(2,1)S(1)} %copy-done.8), custom_call_target="tpu_custom_call" | custom-call | flops 3221225472 | bytes 9437184 | tf_op jit(solution)/shard_map/pallas_call | solution.py:67
  157.1 4.1 %all-to-all-start.1 = ((bf16[4,256,192]{1,2,0:T(8,128)(2,1)}), bf16[4,256,192]{1,2,0:T(8,128)(2,1)}, u32[]{:S(2)}, u32[]{:S(2)}) async-start(bf16[4,256,192]{1,2,0:T(8,128)(2,1)} %copy.17), calls=%async_computation.1 | async-start | bytes 786432 | tf_op jit(solution)/shard_map/all_to_all | solution.py:318
  170.2 15.3 %all-to-all-done.1 = bf16[4,256,192]{1,2,0:T(8,128)(2,1)} async-done(((bf16[4,256,192]{1,2,0:T(8,128)(2,1)}), bf16[4,256,192]{1,2,0:T(8,128)(2,1)}, u32[]{:S(2)}, u32[]{:S(2)}) %all-to-all-start.1) | async-done | bytes 393248 | tf_op jit(solution)/shard_map/all_to_all | solution.py:318
  187.4 8.5 %all-to-all-start.2 = ((bf16[4,256,192]{1,2,0:T(8,128)(2,1)}), bf16[4,256,192]{1,2,0:T(8,128)(2,1)S(1)}, u32[]{:S(2)}, u32[]{:S(2)}) async-start(bf16[4,256,192]{1,2,0:T(8,128)(2,1)} %broadcast_in_dim.58), calls=%async_computation.2 | async-start | bytes 786432 | tf_op jit(solution)/shard_map/all_to_all | solution.py:323
  202.2 14.9 %all-to-all-done.2 = bf16[4,256,192]{1,2,0:T(8,128)(2,1)S(1)} async-done(((bf16[4,256,192]{1,2,0:T(8,128)(2,1)}), bf16[4,256,192]{1,2,0:T(8,128)(2,1)S(1)}, u32[]{:S(2)}, u32[]{:S(2)}) %all-to-all-start.2) | async-done | bytes 393248 | tf_op jit(solution)/shard_map/all_to_all | solution.py:323
  217.3 4.5 %shard_map.129 = bf16[1024,1280]{1,0:T(8,128)(2,1)S(1)} custom-call(bf16[1024,192]{1,0:T(8,128)(2,1)S(1)} %bitcast.70, bf16[1024,2176]{1,0:T(8,128)(2,1)} %bitcast.21.x.marks, bf16[4,64,1024]{2,1,0:T(8,128)(2,1)S(1)} %copy-done.4, bf16[4,64,128]{2,1,0:T(8,128)(2,1)S(1)} %bitcast.73, bf16[4,64,128]{2,1,0:T(8,128)(2,1)S(1)} %bitcast.72), custom_call_target="tpu_custom_call" | custom-call | flops 671088640 | bytes 4194304 | tf_op jit(solution)/shard_map/pallas_call | solution.py:104
  233.6 6.4 %gather_fusion.1 = bf16[4,384,2048]{2,1,0:T(8,128)(2,1)} fusion(bf16[4,384,2048]{2,1,0:T(8,128)(2,1)} %pad_maximum_fusion, s32[1024]{0:T(1024)S(1)} %pad_clamp_fusion), kind=kCustom, calls=%fused_computation.1 | custom fusion | bytes 12582928 | tf_op jit(solution)/shard_map/jit(_take)/gather | solution.py:311
  240.0 13.1 %convolution_bitcast_fusion.refs_2_ = f32[384,1024]{1,0:T(8,128)} fusion(bf16[4,384,2048]{2,1,0:T(8,128)(2,1)} %gather_fusion.1, bf16[4,2048,1024]{2,1,0:T(8,128)(2,1)} %bitcast.74), kind=kOutput, calls=%fused_computation.7 | convolution fusion | flops 6442450944 | bytes 24641536 | tf_op jit(solution)/shard_map/tnf,tfc->nc/dot_general | solution.py:299
  253.1 6.3 %all-to-all-done.3.refs_4_ = bf16[32,32,1280]{2,1,0:T(8,128)(2,1)S(1)} async-done(((bf16[32,32,1280]{2,1,0:T(8,128)(2,1)}), bf16[32,32,1280]{2,1,0:T(8,128)(2,1)S(1)}, u32[]{:S(2)}, u32[]{:S(2)}) %all-to-all-start.3) | async-done | bytes 2621472 | tf_op jit(solution)/shard_map/all_to_all | solution.py:327
  260.7 9.8 %shard_map.130.refs_7_ = bf16[512,1024]{1,0:T(8,128)(2,1)} custom-call(s32[16]{0:T(128)S(1)} %multiply_add_fusion.refs_0_, s32[16]{0:T(128)S(1)} %copy-done.7, f32[384,1024]{1,0:T(8,128)S(1)} %copy-done.3, f32[512,256]{1,0:T(8,128)S(1)} %fusion.1.refs_3_, bf16[32,32,1280]{2,1,0:T(8,128)(2,1)S(1)} %all-to-all-done.3.refs_4_, f32[128,128]{1,0:T(8,128)S(1)} %copy-done.6, ...), custom_call_target="tpu_custom_call" | custom-call | flops 201326592 | bytes 2359296 | tf_op jit(solution)/shard_map/pallas_call | solution.py:184
  270.6 8.3 %convolution_bitcast_fusion.1.refs_2_ = f32[128,1024]{1,0:T(8,128)S(1)} fusion(bf16[4,128,2048]{2,1,0:T(8,128)(2,1)S(1)} %copy-done.9, bf16[4,2048,1024]{2,1,0:T(8,128)(2,1)} %bitcast.75), kind=kOutput, calls=%fused_computation.10 | convolution fusion | flops 2147483648 | bytes 19398656 | tf_op jit(solution)/shard_map/tnf,tfc->nc/dot_general | solution.py:299
  (95 shorter events, 64.8 us)
Async XLA Ops:
  2.0 17.0 %copy-start.2 = (bf16[512,2048]{1,0:T(8,128)(2,1)S(1)}, bf16[512,2048]{1,0:T(8,128)(2,1)}, u32[]{:S(2)}) copy-start(bf16[512,2048]{1,0:T(8,128)(2,1)} %param.13) | copy-start | bytes 6291460
  2.0 81.4 %collective-permute-start = (bf16[128,2048]{1,0:T(8,128)(2,1)}, bf16[128,2048]{1,0:T(8,128)(2,1)}, u32[]{:S(2)}, u32[]{:S(2)}) collective-permute-start(bf16[128,2048]{1,0:T(8,128)(2,1)} %get-tuple-element.14), channel_id=1, source_target_pairs={{0,1},{1,2},{2,3},{4,5},{5,6},{6,7},{8,9},{9,10},{10,11},{12,13},{... | collective-permute-start | bytes 1572872 | tf_op jit(solution)/shard_map/ppermute | solution.py:307
  7.9 76.8 %collective-permute-start.1 = (bf16[128,2048]{1,0:T(8,128)(2,1)}, bf16[128,2048]{1,0:T(8,128)(2,1)}, u32[]{:S(2)}, u32[]{:S(2)}) collective-permute-start(bf16[128,2048]{1,0:T(8,128)(2,1)} %get-tuple-element.14), channel_id=1, source_target_pairs={{1,0},{2,1},{3,2},{5,4},{6,5},{7,6},{9,8},{10,9},{11,10},{13,12},{... | collective-permute-start | bytes 1572872 | tf_op jit(solution)/shard_map/ppermute | solution.py:308
  12.8 73.2 %collective-permute-start.6 = (bf16[384,2048]{1,0:T(8,128)(2,1)}, bf16[384,2048]{1,0:T(8,128)(2,1)}, u32[]{:S(2)}, u32[]{:S(2)}) collective-permute-start(bf16[384,2048]{1,0:T(8,128)(2,1)} %get-tuple-element.12), channel_id=1, source_target_pairs={{0,1},{1,2},{2,3},{4,5},{5,6},{6,7},{8,9},{9,10},{10,11},{12,13},{... | collective-permute-start | bytes 4718600 | tf_op jit(solution)/shard_map/ppermute | solution.py:307
  22.0 125.8 %all-to-all-start = ((bf16[32,32,2176]{2,1,0:T(8,128)(2,1)}), bf16[32,32,2176]{2,1,0:T(8,128)(2,1)}, u32[]{:S(2)}, u32[]{:S(2)}) async-start(bf16[32,32,2176]{2,1,0:T(8,128)(2,1)} %copy-done), calls=%async_computation | async-start | bytes 8912896 | tf_op jit(solution)/shard_map/all_to_all | solution.py:248
  34.8 25.5 %collective-permute-start.12 = (bf16[640,256]{1,0:T(8,128)(2,1)}, bf16[640,256]{1,0:T(8,128)(2,1)S(1)}, u32[]{:S(2)}, u32[]{:S(2)}) collective-permute-start(bf16[640,256]{1,0:T(8,128)(2,1)} %get-tuple-element.15), channel_id=1, source_target_pairs={{0,1},{1,2},{2,3},{3,0},{4,5},{5,6},{6,7},{7,4},{8,9},{9,10},{10,1... | collective-permute-start | bytes 983048 | tf_op jit(solution)/shard_map/ppermute | solution.py:278
  34.8 38.3 %collective-permute-start.14 = (bf16[640,256]{1,0:T(8,128)(2,1)}, bf16[640,256]{1,0:T(8,128)(2,1)S(1)}, u32[]{:S(2)}, u32[]{:S(2)}) collective-permute-start(bf16[640,256]{1,0:T(8,128)(2,1)} %get-tuple-element.16), channel_id=1, source_target_pairs={{0,3},{1,0},{2,1},{3,2},{4,7},{5,4},{6,5},{7,6},{8,11},{9,8},{10,9... | collective-permute-start | bytes 983048 | tf_op jit(solution)/shard_map/ppermute | solution.py:278
  60.4 22.9 %collective-permute-start.13 = (bf16[640,256]{1,0:T(8,128)(2,1)S(1)}, bf16[640,256]{1,0:T(8,128)(2,1)S(1)}, u32[]{:S(2)}, u32[]{:S(2)}) collective-permute-start(bf16[640,256]{1,0:T(8,128)(2,1)S(1)} %get-tuple-element.17), channel_id=1, source_target_pairs={{0,2},{1,3},{2,0},{3,1},{4,6},{5,7},{6,4},{7,5},{8,10},{9,11},{10,... | collective-permute-start | bytes 983048 | tf_op jit(solution)/shard_map/ppermute | solution.py:278
  73.2 46.5 %collective-permute-start.7 = (bf16[384,2048]{1,0:T(8,128)(2,1)}, bf16[384,2048]{1,0:T(8,128)(2,1)}, u32[]{:S(2)}, u32[]{:S(2)}) collective-permute-start(bf16[384,2048]{1,0:T(8,128)(2,1)} %get-tuple-element.12), channel_id=1, source_target_pairs={{1,0},{2,1},{3,2},{5,4},{6,5},{7,6},{9,8},{10,9},{11,10},{13,12},{... | collective-permute-start | bytes 4718600 | tf_op jit(solution)/shard_map/ppermute | solution.py:308
  83.4 14.0 %collective-permute-start.4 = (bf16[128,2048]{1,0:T(8,128)(2,1)}, bf16[128,2048]{1,0:T(8,128)(2,1)S(1)}, u32[]{:S(2)}, u32[]{:S(2)}) collective-permute-start(bf16[128,2048]{1,0:T(8,128)(2,1)} %collective-permute-done), channel_id=1, source_target_pairs={{0,1},{1,2},{2,3},{4,5},{5,6},{6,7},{8,9},{9,10},{10,11},{12,13},{... | collective-permute-start | bytes 1572872 | tf_op jit(solution)/shard_map/ppermute | solution.py:307
  84.7 33.7 %collective-permute-start.2 = (bf16[128,2048]{1,0:T(8,128)(2,1)}, bf16[128,2048]{1,0:T(8,128)(2,1)S(1)}, u32[]{:S(2)}, u32[]{:S(2)}) collective-permute-start(bf16[128,2048]{1,0:T(8,128)(2,1)} %collective-permute-done.1), channel_id=1, source_target_pairs={{1,0},{2,1},{3,2},{5,4},{6,5},{7,6},{9,8},{10,9},{11,10},{13,12},{... | collective-permute-start | bytes 1572872 | tf_op jit(solution)/shard_map/ppermute | solution.py:308
  86.0 56.2 %collective-permute-start.10 = (bf16[384,2048]{1,0:T(8,128)(2,1)}, bf16[384,2048]{1,0:T(8,128)(2,1)}, u32[]{:S(2)}, u32[]{:S(2)}) collective-permute-start(bf16[384,2048]{1,0:T(8,128)(2,1)} %collective-permute-done.6), channel_id=1, source_target_pairs={{0,1},{1,2},{2,3},{4,5},{5,6},{6,7},{8,9},{9,10},{10,11},{12,13},{... | collective-permute-start | bytes 4718600 | tf_op jit(solution)/shard_map/ppermute | solution.py:307
  97.3 43.0 %collective-permute-start.5 = (bf16[128,2048]{1,0:T(8,128)(2,1)S(1)}, bf16[128,2048]{1,0:T(8,128)(2,1)S(1)}, u32[]{:S(2)}, u32[]{:S(2)}) collective-permute-start(bf16[128,2048]{1,0:T(8,128)(2,1)S(1)} %collective-permute-done.4), channel_id=1, source_target_pairs={{0,1},{1,2},{2,3},{4,5},{5,6},{6,7},{8,9},{9,10},{10,11},{12,13},{... | collective-permute-start | bytes 1572872 | tf_op jit(solution)/shard_map/ppermute | solution.py:307
  118.4 42.8 %collective-permute-start.3 = (bf16[128,2048]{1,0:T(8,128)(2,1)S(1)}, bf16[128,2048]{1,0:T(8,128)(2,1)S(1)}, u32[]{:S(2)}, u32[]{:S(2)}) collective-permute-start(bf16[128,2048]{1,0:T(8,128)(2,1)S(1)} %collective-permute-done.2), channel_id=1, source_target_pairs={{1,0},{2,1},{3,2},{5,4},{6,5},{7,6},{9,8},{10,9},{11,10},{13,12},{... | collective-permute-start | bytes 1572872 | tf_op jit(solution)/shard_map/ppermute | solution.py:308
  119.7 45.6 %collective-permute-start.8 = (bf16[384,2048]{1,0:T(8,128)(2,1)}, bf16[384,2048]{1,0:T(8,128)(2,1)}, u32[]{:S(2)}, u32[]{:S(2)}) collective-permute-start(bf16[384,2048]{1,0:T(8,128)(2,1)} %collective-permute-done.7), channel_id=1, source_target_pairs={{1,0},{2,1},{3,2},{5,4},{6,5},{7,6},{9,8},{10,9},{11,10},{13,12},{... | collective-permute-start | bytes 4718600 | tf_op jit(solution)/shard_map/ppermute | solution.py:308
  142.2 56.8 %collective-permute-start.11 = (bf16[384,2048]{1,0:T(8,128)(2,1)}, bf16[384,2048]{1,0:T(8,128)(2,1)}, u32[]{:S(2)}, u32[]{:S(2)}) collective-permute-start(bf16[384,2048]{1,0:T(8,128)(2,1)} %collective-permute-done.10), channel_id=1, source_target_pairs={{0,1},{1,2},{2,3},{4,5},{5,6},{6,7},{8,9},{9,10},{10,11},{12,13},{... | collective-permute-start | bytes 4718600 | tf_op jit(solution)/shard_map/ppermute | solution.py:307
  157.1 28.4 %all-to-all-start.1 = ((bf16[4,256,192]{1,2,0:T(8,128)(2,1)}), bf16[4,256,192]{1,2,0:T(8,128)(2,1)}, u32[]{:S(2)}, u32[]{:S(2)}) async-start(bf16[4,256,192]{1,2,0:T(8,128)(2,1)} %copy.17), calls=%async_computation.1 | async-start | bytes 786432 | tf_op jit(solution)/shard_map/all_to_all | solution.py:318
  165.3 61.8 %collective-permute-start.9 = (bf16[384,2048]{1,0:T(8,128)(2,1)}, bf16[384,2048]{1,0:T(8,128)(2,1)}, u32[]{:S(2)}, u32[]{:S(2)}) collective-permute-start(bf16[384,2048]{1,0:T(8,128)(2,1)} %collective-permute-done.8), channel_id=1, source_target_pairs={{1,0},{2,1},{3,2},{5,4},{6,5},{7,6},{9,8},{10,9},{11,10},{13,12},{... | collective-permute-start | bytes 4718600 | tf_op jit(solution)/shard_map/ppermute | solution.py:308
  187.4 29.8 %all-to-all-start.2 = ((bf16[4,256,192]{1,2,0:T(8,128)(2,1)}), bf16[4,256,192]{1,2,0:T(8,128)(2,1)S(1)}, u32[]{:S(2)}, u32[]{:S(2)}) async-start(bf16[4,256,192]{1,2,0:T(8,128)(2,1)} %broadcast_in_dim.58), calls=%async_computation.2 | async-start | bytes 786432 | tf_op jit(solution)/shard_map/all_to_all | solution.py:323
  199.0 18.3 %copy-start.4 = (bf16[4,64,1024]{2,1,0:T(8,128)(2,1)S(1)}, bf16[4,64,1024]{2,1,0:T(8,128)(2,1)}, u32[]{:S(2)}) copy-start(bf16[4,64,1024]{2,1,0:T(8,128)(2,1)} %wq.1) | copy-start | bytes 1572868
  223.3 36.0 %all-to-all-start.3 = ((bf16[32,32,1280]{2,1,0:T(8,128)(2,1)}), bf16[32,32,1280]{2,1,0:T(8,128)(2,1)S(1)}, u32[]{:S(2)}, u32[]{:S(2)}) async-start(bf16[32,32,1280]{2,1,0:T(8,128)(2,1)} %bitcast.68), calls=%async_computation.3 | async-start | bytes 5242880 | tf_op jit(solution)/shard_map/all_to_all | solution.py:327
  240.0 19.3 %copy-start.5 = (f32[128,128]{1,0:T(8,128)S(1)}, f32[128,128]{1,0:T(8,128)}, u32[]{:S(2)}) copy-start(f32[128,128]{1,0:T(8,128)} %constant.128.clone.refs_6_) | copy-start | bytes 196612
  240.0 19.3 %copy-start.6 = (f32[128,128]{1,0:T(8,128)S(1)}, f32[128,128]{1,0:T(8,128)}, u32[]{:S(2)}) copy-start(f32[128,128]{1,0:T(8,128)} %constant.127.clone.refs_5_) | copy-start | bytes 196612
  240.0 19.3 %copy-start.7 = (s32[16]{0:T(128)S(1)}, s32[16]{0:T(128)}, u32[]{:S(2)}) copy-start(s32[16]{0:T(128)} %refs_1_.3) | copy-start | bytes 196
  (12 other events, 73.8 us)
